TPU v7x, 256 devices: a whole 4x4x8 slice. The times are simulated.
256 devices in a mesh: env: 32 (over x, z), cand: 8 (over y, core).
Axes of the slice: x: 4, y: 4, z: 8, core: 2. Of those that a mesh axis runs over, the one named last changes fastest.
Arguments:
- params: bfloat16 [346880], P(('env', 'cand')), may hold values from -6 to 6
- h_start: float32 [64, 200], P('env'), may hold values from -1 to 1
- z_start: float32 [64, 30], P('env'), may hold values from -5 to 5
- action_noise: bfloat16 [3, 12, 6, 64, 1024], P(None, None, None, 'env', 'cand'), may hold values from -4 to 4
- state_noise: bfloat16 [3, 12, 30, 64, 1024], P(None, None, None, 'env', 'cand'), may hold values from -4 to 4
- elites: int32 [3, 64, 100], P(None, 'env'), may hold values from 0 to 1023, as said below
Outputs:
- plan_mean: float32 [12, 6, 64], P(None, None, 'env')
- plan_spread: float32 [12, 6, 64], P(None, None, 'env')
- returns: float32 [3, 64, 1024], P(None, 'env', 'cand')
- best_return: float32 [3, 64], P(None, 'env')
Inputs may be any that keep to these rules, and one draw needn't show every extreme that they name: `elites`: for each iteration and environment, 100 different candidate numbers.
All inputs are finite; a program needn't handle non-finite values.
Results may differ from a plain program's by a relative error of at most 0.0065.
Values may be sent and summed in bfloat16 or wider, within the bound.
No kernel may reach another device: no remote copies, remote signals or barrier semaphores. Data moves between devices by JAX's collectives and lax.ppermute only.
A program may use at most 64 MiB of HBM per device.

v0:
```python
import jax
import jax.numpy as jnp
from jax import lax
from jax.sharding import PartitionSpec as P

D_DET = 200
STOCH = 30
HID = 200
ACT = 6
HOR = 12
ITERS = 3


bias_scale = 0.2
min_scale = 0.1
variance_floor = 1e-05


def from_everyone(shard, axis):
    peers = lax.axis_size(axis)
    return lax.all_to_all(
        jnp.broadcast_to(shard[None], (peers, *shard.shape)), axis, 0, 0, tiled=True
    )


def in_order(parts, dim):
    parts = jnp.moveaxis(parts, 0, dim)
    shape = parts.shape
    return parts.reshape(*shape[:dim], shape[dim] * shape[dim + 1], *shape[dim + 2 :])


def gathered_copies(shard, axis, dim):
    parts = from_everyone(shard, axis)
    return in_order(parts, dim)


def of_everyone(shard, axis):
    return from_everyone(shard, axis).max(axis=0)


def in_one(arrays, axis):
    ends = [0]
    for a in arrays:
        ends.append(ends[-1] + a.size)
    subtotal = of_everyone(jnp.concatenate([a.ravel() for a in arrays]), axis)
    return tuple((subtotal[b:e].reshape(a.shape) for a, b, e in zip(arrays, ends, ends[1:])))


def taken_together(shard, axis):
    everything = from_everyone(shard, axis)
    return jnp.sum(everything, axis=0)


def packed_total(arrays, axis):
    ends = [0]
    for a in arrays:
        ends.append(ends[-1] + a.size)
    subtotal = taken_together(jnp.concatenate([a.ravel() for a in arrays]), axis)
    return tuple((subtotal[b:e].reshape(a.shape) for a, b, e in zip(arrays, ends, ends[1:])))


def split_params(flat_params):
    layer_shapes = [
        (STOCH + ACT, HID),
        (HID + D_DET, 2 * D_DET),
        (HID + D_DET, D_DET),
        (D_DET, HID),
        (HID, 2 * STOCH),
        (D_DET + STOCH, HID),
        (HID, 1),
    ]
    offset = 0
    layers = []
    for fan_in, fan_out in layer_shapes:
        matrix = flat_params[offset : offset + fan_in * fan_out].reshape(fan_in, fan_out)
        offset = offset + fan_in * fan_out
        biases = flat_params[offset : offset + fan_out]
        offset = offset + fan_out
        layers.append((matrix.T, biases.astype(jnp.float32) * bias_scale, fan_in ** (-0.5)))
    return layers


def affine(layer, inputs):
    matrix_t, biases, factor = layer
    return jnp.dot(matrix_t, inputs, preferred_element_type=jnp.float32) * factor + biases[:, None]


def rollout(layers, start_state, start_latent, action_seq, noise_seq):

    def advance(carried, inputs):
        state, latent, return_sum = carried
        action, sample_noise = inputs
        joined = jnp.concatenate([latent, action], 0).astype(jnp.bfloat16)
        embedded = jax.nn.elu(affine(layers[0], joined)).astype(jnp.bfloat16)
        gate_values = jax.nn.sigmoid(
            affine(layers[1], jnp.concatenate([embedded, state.astype(jnp.bfloat16)], 0))
        )
        reset_gate = gate_values[:D_DET]
        update = gate_values[D_DET:]
        proposal = jnp.tanh(
            affine(
                layers[2], jnp.concatenate([embedded, (reset_gate * state).astype(jnp.bfloat16)], 0)
            )
        )
        next_state = update * state + (1.0 - update) * proposal
        state_low = next_state.astype(jnp.bfloat16)
        prior_hidden = jax.nn.elu(affine(layers[3], state_low)).astype(jnp.bfloat16)
        prior_stats = affine(layers[4], prior_hidden)
        prior_scale = jax.nn.softplus(prior_stats[STOCH:]) + min_scale
        next_latent = prior_stats[:STOCH] + prior_scale * sample_noise.astype(jnp.float32)
        reward_hidden = jax.nn.elu(
            affine(layers[5], jnp.concatenate([state_low, next_latent.astype(jnp.bfloat16)], 0))
        ).astype(jnp.bfloat16)
        reward = affine(layers[6], reward_hidden)[0]
        return ((next_state, next_latent, return_sum + reward), None)

    initial = (start_state, start_latent, jnp.zeros(start_state.shape[1], jnp.float32))
    final, _ = lax.scan(advance, initial, (action_seq, noise_seq))
    return final[2]


def body(params, h_start, z_start, action_noise, state_noise, elites):
    group_params = gathered_copies(params, "cand", 0)
    flat_params = gathered_copies(group_params, "env", 0)
    layers = split_params(flat_params)
    envs_here = h_start.shape[0]
    cands_here = action_noise.shape[4]
    row_count = envs_here * cands_here
    start_state = jnp.broadcast_to(h_start.T[:, :, None], (D_DET, envs_here, cands_here)).reshape(
        D_DET, row_count
    )
    start_latent = jnp.broadcast_to(z_start.T[:, :, None], (STOCH, envs_here, cands_here)).reshape(
        STOCH, row_count
    )
    candidate_ids = lax.axis_index("cand") * cands_here + jnp.arange(cands_here, dtype=jnp.int32)
    center = jnp.zeros((HOR, ACT, envs_here), jnp.float32)
    spread = jnp.ones((HOR, ACT, envs_here), jnp.float32)
    totals = []
    best_values = []
    for number in range(ITERS):
        actions = center[..., None] + spread[..., None] * action_noise[number].astype(jnp.float32)
        return_sum = rollout(
            layers,
            start_state,
            start_latent,
            actions.reshape(HOR, ACT, row_count),
            state_noise[number].reshape(HOR, STOCH, row_count),
        )
        return_grid = return_sum.reshape(envs_here, cands_here)
        totals.append(return_grid)
        matches = elites[number][:, :, None] == candidate_ids[None, None, :]
        best, negated = in_one(
            (jnp.max(return_grid, axis=1), -jnp.min(return_grid, axis=1)), "cand"
        )
        best_values.append(best)
        chosen = jnp.any(matches, axis=1).astype(jnp.float32)
        weight = chosen * (return_grid + negated[:, None] + 1.0)
        weighted = actions * weight[None, None]
        total, moment_one, squares = packed_total(
            (
                jnp.sum(weight, axis=1),
                jnp.sum(weighted, axis=3),
                jnp.sum(weighted * actions, axis=3),
            ),
            "cand",
        )
        center = moment_one / total[None, None]
        spread = jnp.sqrt(
            jnp.maximum(squares / total[None, None] - center * center, 0.0) + variance_floor
        )
    return (center, spread, jnp.stack(totals), jnp.stack(best_values))


def solution(mesh):
    placed = (
        P(("env", "cand")),
        P("env", None),
        P("env", None),
        P(None, None, None, "env", "cand"),
        P(None, None, None, "env", "cand"),
        P(None, "env", None),
    )
    return jax.shard_map(
        body,
        mesh=mesh,
        in_specs=placed,
        out_specs=(
            P(None, None, "env"),
            P(None, None, "env"),
            P(None, "env", "cand"),
            P(None, "env"),
        ),
        check_vma=False,
    )
```

profile of v0, /device:TPU:1, one launch (start us, length us, event | category | flops | bytes accessed | tf_op | source)
XLA Modules:
  0.0 195.3 jit_solution(3518255296276274576)
XLA Ops:
  0.6 0.7 broadcast_in_dim.42
  1.3 10.5 %all_to_all.48 = bf16[8,1,1355]{2,1,0:T(2,128)(2,1)S(1)} all-to-all(bf16[8,1,1355]{2,1,0:T(2,128)(2,1)S(1)} %broadcast_in_dim.42), channel_id=1, replica_groups=mesh['env'=32,'cand'=8] {'cand'}, dimensions={0} | all-to-all | bytes 43360 | tf_op jit(solution)/shard_map/all_to_all | solution.py:21
  12.1 0.7 broadcast_in_dim.44
  13.4 5.0 %reduce.8 = bf16[32,10840]{1,0:T(8,128)(2,1)S(1)} reduce(bf16[32,1,10840]{2,1,0:T(2,128)(2,1)S(1)} %broadcast_in_dim.44, bf16[]{:T(256)} %broadcast.462), dimensions={1}, to_apply=%broadcast_in_dim.44.reduce_sub_computation | reduce | bytes 1387522 | tf_op jit(solution)/shard_map/broadcast_in_dim | solution.py:22
  18.4 1.6 reshape.363
  20.0 11.3 %all-to-all-start.1 = ((bf16[32,2,5420]{2,1,0:T(2,128)(2,1)}), bf16[32,2,5420]{2,1,0:T(2,128)(2,1)S(1)}, u32[]{:S(2)}, u32[]{:S(2)}) async-start(bf16[32,2,5420]{2,1,0:T(2,128)(2,1)} %reshape.363), calls=%async_computation.1 | async-start | bytes 1409024 | tf_op jit(solution)/shard_map/all_to_all | solution.py:21
  32.4 0.7 reshape.340
  35.0 14.1 %all-to-all-done.1 = bf16[32,2,5420]{2,1,0:T(2,128)(2,1)S(1)} async-done(((bf16[32,2,5420]{2,1,0:T(2,128)(2,1)}), bf16[32,2,5420]{2,1,0:T(2,128)(2,1)S(1)}, u32[]{:S(2)}, u32[]{:S(2)}) %all-to-all-start.1) | async-done | bytes 693792 | tf_op jit(solution)/shard_map/all_to_all | solution.py:21
  49.1 0.9 reshape.364
  50.0 4.6 %reduce.7 = bf16[32,10840]{1,0:T(8,128)(2,1)S(1)} reduce(bf16[32,1,10840]{2,1,0:T(2,128)(2,1)S(1)} %reshape.364, bf16[]{:T(256)} %constant.135), dimensions={1}, to_apply=%all_to_all.33.reduce_sub_computation | reduce | bytes 1387522 | tf_op jit(solution)/shard_map/all_to_all | solution.py:21
  54.5 1.1 reshape.315
  56.5 0.7 slice.225
  57.2 0.9 reshape.317
  58.3 0.6 reshape.318
  61.3 28.6 %while.45 = (s32[]{:T(128)}, f32[200,256]{1,0:T(8,128)S(1)}, bf16[30,256]{1,0:T(8,128)(2,1)S(1)}, f32[256]{0:T(256)S(1)}, bf16[12,6,256]{2,1,0:T(8,128)(2,1)}, /...) while((s32[]{:T(128)}, f32[200,256]{1,0:T(8,128)S(1)}, ...), condition=%wide.region_4.5_spmd.clone, body=%wide.region_3.4_spmd.clone.sunk | while | flops 179998208 | bytes 3556091 | solution.py:118
  61.3 0.7 fusion.284
  63.7 0.7 fusion.284
  66.1 0.7 fusion.284
  68.5 0.7 fusion.284
  70.8 0.7 fusion.284
  73.2 0.7 fusion.284
  75.6 0.7 fusion.284
  78.0 0.7 fusion.284
  80.3 0.7 fusion.284
  82.7 0.7 fusion.284
  85.1 0.7 fusion.284
  87.5 0.7 fusion.284
  90.1 0.6 broadcast_in_dim.45
  90.7 7.9 %all-to-all-start.2 = ((f32[8,1,4]{2,1,0:T(1,128)}), f32[8,1,4]{2,1,0:T(1,128)S(1)}, u32[]{:S(2)}, u32[]{:S(2)}) async-start(f32[8,1,4]{2,1,0:T(1,128)} %broadcast_in_dim.45), calls=%async_computation.2 | async-start | bytes 8192 | tf_op jit(solution)/shard_map/all_to_all | solution.py:21
  98.8 4.3 %all-to-all-done.2 = f32[8,1,4]{2,1,0:T(1,128)S(1)} async-done(((f32[8,1,4]{2,1,0:T(1,128)}), f32[8,1,4]{2,1,0:T(1,128)S(1)}, u32[]{:S(2)}, u32[]{:S(2)}) %all-to-all-start.2) | async-done | bytes 160 | tf_op jit(solution)/shard_map/all_to_all | solution.py:21
  104.0 0.6 broadcast_in_dim.46
  104.6 3.9 %all-to-all-start.3 = ((f32[8,1,290]{2,1,0:T(1,128)}), f32[8,1,290]{2,1,0:T(1,128)S(1)}, u32[]{:S(2)}, u32[]{:S(2)}) async-start(f32[8,1,290]{2,1,0:T(1,128)} %broadcast_in_dim.46), calls=%async_computation.3 | async-start | bytes 24576 | tf_op jit(solution)/shard_map/all_to_all | solution.py:21
  108.7 4.4 %all-to-all-done.3 = f32[8,1,290]{2,1,0:T(1,128)S(1)} async-done(((f32[8,1,290]{2,1,0:T(1,128)}), f32[8,1,290]{2,1,0:T(1,128)S(1)}, u32[]{:S(2)}, u32[]{:S(2)}) %all-to-all-start.3) | async-done | bytes 9312 | tf_op jit(solution)/shard_map/all_to_all | solution.py:21
  114.0 20.4 %while.46 = (s32[]{:T(128)}, f32[200,256]{1,0:T(8,128)S(1)}, bf16[30,256]{1,0:T(8,128)(2,1)S(1)}, f32[256]{0:T(256)S(1)}, bf16[12,6,256]{2,1,0:T(8,128)(2,1)S(1)...) while((s32[]{:T(128)}, f32[200,256]{1,0:T(8,128)S(1)}, ...), condition=%wide.region_13.14_spmd.clone, body=%wide.region_12.13_spmd.clone.sunk | while | flops 179998208 | bytes 3556091 | solution.py:118
  134.7 7.6 %all_to_all.49 = f32[8,1,4]{2,1,0:T(1,128)S(1)} all-to-all(f32[8,1,4]{2,1,0:T(1,128)S(1)} %broadcast_in_dim.47), channel_id=1, replica_groups=mesh['env'=32,'cand'=8] {'cand'}, dimensions={0} | all-to-all | bytes 256 | tf_op jit(solution)/shard_map/all_to_all | solution.py:21
  143.4 0.6 broadcast_in_dim.48
  144.0 3.9 %all-to-all-start.5 = ((f32[8,1,290]{2,1,0:T(1,128)}), f32[8,1,290]{2,1,0:T(1,128)S(1)}, u32[]{:S(2)}, u32[]{:S(2)}) async-start(f32[8,1,290]{2,1,0:T(1,128)} %broadcast_in_dim.48), calls=%async_computation.5 | async-start | bytes 24576 | tf_op jit(solution)/shard_map/all_to_all | solution.py:21
  148.1 4.5 %all-to-all-done.5 = f32[8,1,290]{2,1,0:T(1,128)S(1)} async-done(((f32[8,1,290]{2,1,0:T(1,128)}), f32[8,1,290]{2,1,0:T(1,128)S(1)}, u32[]{:S(2)}, u32[]{:S(2)}) %all-to-all-start.5) | async-done | bytes 9312 | tf_op jit(solution)/shard_map/all_to_all | solution.py:21
  153.5 20.4 %while.47 = (s32[]{:T(128)}, f32[200,256]{1,0:T(8,128)S(1)}, bf16[30,256]{1,0:T(8,128)(2,1)S(1)}, f32[256]{0:T(256)S(1)}, bf16[12,6,256]{2,1,0:T(8,128)(2,1)S(1)...) while((s32[]{:T(128)}, f32[200,256]{1,0:T(8,128)S(1)}, ...), condition=%wide.region_22.23_spmd.clone, body=%wide.region_21.22_spmd.clone.sunk | while | flops 179998208 | bytes 3556091 | solution.py:118
  174.2 0.6 broadcast_in_dim.49
  174.8 3.9 %all-to-all-start.6 = ((f32[8,1,4]{2,1,0:T(1,128)}), f32[8,1,4]{2,1,0:T(1,128)S(1)}, u32[]{:S(2)}, u32[]{:S(2)}) async-start(f32[8,1,4]{2,1,0:T(1,128)} %broadcast_in_dim.49), calls=%async_computation.6 | async-start | bytes 8192 | tf_op jit(solution)/shard_map/all_to_all | solution.py:21
  179.3 3.9 %all-to-all-done.6 = f32[8,1,4]{2,1,0:T(1,128)S(1)} async-done(((f32[8,1,4]{2,1,0:T(1,128)}), f32[8,1,4]{2,1,0:T(1,128)S(1)}, u32[]{:S(2)}, u32[]{:S(2)}) %all-to-all-start.6) | async-done | bytes 160 | tf_op jit(solution)/shard_map/all_to_all | solution.py:21
  184.3 0.6 broadcast_in_dim.50
  184.9 3.9 %all-to-all-start.7 = ((f32[8,1,290]{2,1,0:T(1,128)}), f32[8,1,290]{2,1,0:T(1,128)S(1)}, u32[]{:S(2)}, u32[]{:S(2)}) async-start(f32[8,1,290]{2,1,0:T(1,128)} %broadcast_in_dim.50), calls=%async_computation.7 | async-start | bytes 24576 | tf_op jit(solution)/shard_map/all_to_all | solution.py:21
  188.8 0.6 copy.114
  189.5 4.0 %all-to-all-done.7 = f32[8,1,290]{2,1,0:T(1,128)S(1)} async-done(((f32[8,1,290]{2,1,0:T(1,128)}), f32[8,1,290]{2,1,0:T(1,128)S(1)}, u32[]{:S(2)}, u32[]{:S(2)}) %all-to-all-start.7) | async-done | bytes 9312 | tf_op jit(solution)/shard_map/all_to_all | solution.py:21
  193.9 0.7 copy.112
  194.6 0.7 copy.113
  (477 shorter events, 72.7 us)
Async XLA Ops:
  18.4 13.0 %copy-start = (bf16[3,12,30,2,128]{4,3,2,1,0:T(2,128)(2,1)S(1)}, bf16[3,12,30,2,128]{4,3,2,1,0:T(2,128)(2,1)}, u32[]{:S(2)}) copy-start(bf16[3,12,30,2,128]{4,3,2,1,0:T(2,128)(2,1)} %param.16) | copy-start | bytes 1658884
  19.9 11.9 %copy-start.7 = (f32[2,200]{1,0:T(2,128)S(1)}, f32[2,200]{1,0:T(2,128)}, u32[]{:S(2)}) copy-start(f32[2,200]{1,0:T(2,128)} %param.13) | copy-start | bytes 4804
  20.0 29.1 %all-to-all-start.1 = ((bf16[32,2,5420]{2,1,0:T(2,128)(2,1)}), bf16[32,2,5420]{2,1,0:T(2,128)(2,1)S(1)}, u32[]{:S(2)}, u32[]{:S(2)}) async-start(bf16[32,2,5420]{2,1,0:T(2,128)(2,1)} %reshape.363), calls=%async_computation.1 | async-start | bytes 1409024 | tf_op jit(solution)/shard_map/all_to_all | solution.py:21
  31.3 1.0 copy-start.1
  31.3 1.8 copy-start.8
  31.4 3.1 %copy-start.6 = (s32[3,2,100]{2,1,0:T(2,128)S(1)}, s32[3,2,100]{2,1,0:T(2,128)}, u32[]{:S(2)}) copy-start(s32[3,2,100]{2,1,0:T(2,128)} %param.17) | copy-start | bytes 7204
  58.1 3.1 %copy-start.2 = (bf16[30,256]{1,0:T(8,128)(2,1)S(1)}, bf16[30,256]{1,0:T(8,128)(2,1)}, u32[]{:S(2)}) copy-start(bf16[30,256]{1,0:T(8,128)(2,1)} %copy.142) | copy-start | bytes 46084
  61.3 37.3 %copy-start.3 = (s32[2,100]{1,0:T(2,128)S(1)}, s32[2,100]{1,0:T(2,128)}, u32[]{:S(2)}) copy-start(s32[2,100]{1,0:T(2,128)} %get-tuple-element.925) | copy-start | bytes 2404
  61.3 37.3 %copy-start.4 = (s32[2,100]{1,0:T(2,128)S(1)}, s32[2,100]{1,0:T(2,128)}, u32[]{:S(2)}) copy-start(s32[2,100]{1,0:T(2,128)} %get-tuple-element.926) | copy-start | bytes 2404
  61.3 37.3 %copy-start.5 = (s32[2,100]{1,0:T(2,128)S(1)}, s32[2,100]{1,0:T(2,128)}, u32[]{:S(2)}) copy-start(s32[2,100]{1,0:T(2,128)} %get-tuple-element.927) | copy-start | bytes 2404
  61.3 37.3 %copy-start.9 = (s32[128]{0:T(128)S(1)}, s32[128]{0:T(128)}, u32[]{:S(2)}) copy-start(s32[128]{0:T(128)} %iota_add_fusion) | copy-start | bytes 1540
  90.7 12.4 %all-to-all-start.2 = ((f32[8,1,4]{2,1,0:T(1,128)}), f32[8,1,4]{2,1,0:T(1,128)S(1)}, u32[]{:S(2)}, u32[]{:S(2)}) async-start(f32[8,1,4]{2,1,0:T(1,128)} %broadcast_in_dim.45), calls=%async_computation.2 | async-start | bytes 8192 | tf_op jit(solution)/shard_map/all_to_all | solution.py:21
  104.6 8.6 %all-to-all-start.3 = ((f32[8,1,290]{2,1,0:T(1,128)}), f32[8,1,290]{2,1,0:T(1,128)S(1)}, u32[]{:S(2)}, u32[]{:S(2)}) async-start(f32[8,1,290]{2,1,0:T(1,128)} %broadcast_in_dim.46), calls=%async_computation.3 | async-start | bytes 24576 | tf_op jit(solution)/shard_map/all_to_all | solution.py:21
  144.0 8.6 %all-to-all-start.5 = ((f32[8,1,290]{2,1,0:T(1,128)}), f32[8,1,290]{2,1,0:T(1,128)S(1)}, u32[]{:S(2)}, u32[]{:S(2)}) async-start(f32[8,1,290]{2,1,0:T(1,128)} %broadcast_in_dim.48), calls=%async_computation.5 | async-start | bytes 24576 | tf_op jit(solution)/shard_map/all_to_all | solution.py:21
  174.8 8.4 %all-to-all-start.6 = ((f32[8,1,4]{2,1,0:T(1,128)}), f32[8,1,4]{2,1,0:T(1,128)S(1)}, u32[]{:S(2)}, u32[]{:S(2)}) async-start(f32[8,1,4]{2,1,0:T(1,128)} %broadcast_in_dim.49), calls=%async_computation.6 | async-start | bytes 8192 | tf_op jit(solution)/shard_map/all_to_all | solution.py:21
  184.9 8.6 %all-to-all-start.7 = ((f32[8,1,290]{2,1,0:T(1,128)}), f32[8,1,290]{2,1,0:T(1,128)S(1)}, u32[]{:S(2)}, u32[]{:S(2)}) async-start(f32[8,1,290]{2,1,0:T(1,128)} %broadcast_in_dim.50), calls=%async_computation.7 | async-start | bytes 24576 | tf_op jit(solution)/shard_map/all_to_all | solution.py:21
where the time goes:
time: 196 us; the launch traced here: 195 us
  matrix products  55.7 us (28%)
  waiting for transfers between devices  35.2 us (18%)
  starting transfers between devices  34.9 us (18%)
  local copies, waits for them, and re-layouts  29.9 us (15%)
  blocking collectives  18.2 us (9%)
  other arithmetic  17.8 us (9%)
    dot_general x180, matrix products, affine(): jnp.dot(matrix_t, inputs, preferred_element_type=jnp.float32) * factor  55.7 us
    all_to_all x6, waiting for transfers between devices, from_everyone(): lax.all_to_all(jnp.broadcast_to(shard[None], (peers, *shard.shape)), axis...  35.2 us
    all_to_all x6, starting transfers between devices, from_everyone(): lax.all_to_all(jnp.broadcast_to(shard[None], (peers, *shard.shape)), axis...  34.9 us
    all_to_all x2, blocking collectives, from_everyone(): lax.all_to_all(jnp.broadcast_to(shard[None], (peers, *shard.shape)), axis...  18.2 us
    squeeze x36, local copies, waits for them, and re-layouts, rollout(): final, _ = lax.scan(advance, initial, (action_seq, noise_seq))  8.3 us
    unnamed x38, local copies, waits for them, and re-layouts  5.98 us
    broadcast_in_dim x10, local copies, waits for them, and re-layouts, from_everyone(): jnp.broadcast_to(shard[None], (peers, *shard.shape))  5.11 us
    broadcast_in_dim x1, other arithmetic, from_everyone(): jnp.broadcast_to(shard[None], (peers, *shard.shape))  5 us
  transfers between devices with their start and end apart: 6, of which 6 were waited for; matrix products, arithmetic and copies ran while one was open for 3% of the time, Pallas kernels for 0%

commit v1 on v0

v1 whole, which is shorter than its diff:
```python
import functools

import jax
import jax.numpy as jnp
from jax import lax
from jax.experimental import pallas as pl
from jax.experimental.pallas import tpu as pltpu
from jax.sharding import PartitionSpec as P

D_DET = 200
STOCH = 30
HID = 200
ACT = 6
HOR = 12
ITERS = 3

PEERS = 8
ENVS_HERE = 2
CANDS_HERE = 128
COLS = ENVS_HERE * CANDS_HERE

WIDE = 208
DEEP = 256
ROWS = 96
ONE = 96

bias_scale = 0.2
min_scale = 0.1
variance_floor = 1e-05

S36, S400, S200, S230 = (float(n) ** -0.5 for n in (36, 400, 200, 230))
LOG2E = 1.4426950408889634

F32, BF16 = jnp.float32, jnp.bfloat16


def dot(a, b):
    return jnp.dot(a, b, preferred_element_type=F32)


def scaled_elu(y, scale):
    return jnp.where(y > 0, y * scale, jnp.exp2(y * (scale * LOG2E)) - 1.0)


def softplus(v):
    return jnp.maximum(v, 0.0) + jnp.log(1.0 + jnp.exp(-jnp.abs(v)))


def refit(state, gathered):
    rows = []
    best = []
    for e in range(ENVS_HERE):
        m1, c1, m2, c2 = (gathered[:, 4 * e + k, :] for k in range(4))
        lowest = c1[:, ONE + 2 : ONE + 3]
        highest = c1[:, ONE + 1 : ONE + 2]
        worst = jnp.min(lowest, axis=0, keepdims=True)
        best.append(jnp.max(highest, axis=0, keepdims=True))
        lift = lowest - worst
        m1 = jnp.sum(m1 + lift * c1, axis=0, keepdims=True)
        m2 = jnp.sum(m2 + lift * c2, axis=0, keepdims=True)
        total = m1[:, ONE : ONE + 1]
        m1 = m1 / total
        m2 = m2 / total
        center = state[2 * e : 2 * e + 1]
        spread = state[2 * e + 1 : 2 * e + 2]
        rows.append(center + spread * m1)
        rows.append(
            jnp.sqrt(spread * spread * jnp.maximum(m2 - m1 * m1, 0.0) + variance_floor)
        )
    state = jnp.concatenate(rows + [jnp.zeros((4, 128), F32)], 0)
    return state, jnp.concatenate([jnp.broadcast_to(b, (1, 128)) for b in best], 0)


def split(v):
    hi = v.astype(BF16)
    return hi, v - hi.astype(F32)


def rollout_kernel(
    first, number, w_h, w_x, w_za, w_r, w_p, w_7, h0, z0, a_noise, s_noise, chosen, *rest
):
    if first:
        ret_ref, msg_ref, acts, h_ref, q_ref = rest
    else:
        state_ref, got_ref, ret_ref, msg_ref, new_state_ref, best_ref, acts, h_ref, q_ref = rest
    noise = a_noise[number].astype(F32)
    if first:
        acts[...] = noise
    else:
        state, best = refit(state_ref[...], got_ref[...])
        new_state_ref[...] = state
        best_ref[...] = best
        columns = jnp.transpose(state)
        for e in range(ENVS_HERE):
            at = pl.ds(e * CANDS_HERE, CANDS_HERE)
            center = columns[:ROWS, 2 * e : 2 * e + 1]
            spread = columns[:ROWS, 2 * e + 1 : 2 * e + 2]
            acts[:, at] = center + spread * noise[:, e * CANDS_HERE : (e + 1) * CANDS_HERE]
    rows8 = lax.broadcasted_iota(jnp.int32, (8, COLS), 0)
    ones8 = jnp.where(rows8 < 2, 1.0, 0.0).astype(F32)
    ones48 = jnp.concatenate([ones8, jnp.zeros((DEEP - WIDE - 8, COLS), F32)], 0).astype(BF16)

    def deep(v):
        return jnp.concatenate([v.astype(BF16), ones48], 0)

    h_ref[...] = h0[...]
    q_ref[...] = jnp.zeros_like(q_ref)

    def step(t, z):
        h = h_ref[...]
        hd = deep(h)
        gates_h = dot(w_h[: 2 * WIDE], hd)
        za = jnp.concatenate([z, acts[pl.ds(pl.multiple_of(t * 8, 8), 8), :], ones8], 0).astype(BF16)
        x = deep(scaled_elu(dot(w_za[:WIDE], za), S36))
        gates = dot(w_x[: 2 * WIDE], x) + gates_h
        reset = jnp.tanh(gates[:WIDE] * (0.5 * S400))
        half = 0.5 * h
        rh = deep(half + reset * half)
        proposal = jnp.tanh((dot(w_x[2 * WIDE :], x) + dot(w_r[...], rh)) * S400)
        update = 0.5 + 0.5 * jnp.tanh(gates[WIDE:] * (0.5 * S400))
        h = proposal + update * (h - proposal)
        h_ref[...] = h
        hd = deep(h)
        p = deep(scaled_elu(dot(w_h[2 * WIDE : 3 * WIDE], hd), S200))
        s = dot(w_p[...], p) * S200
        scale = softplus(s[32:]) + min_scale
        z = s[:32] + scale * s_noise[number, t].astype(F32)
        zb = jnp.concatenate([z, jnp.zeros((16, COLS), F32)], 0).astype(BF16)
        q = scaled_elu(dot(w_h[3 * WIDE :], hd) + dot(w_za[WIDE:], zb), S230)
        q_ref[...] += q.astype(BF16).astype(F32)
        return z

    lax.fori_loop(0, HOR, step, z0[...])

    total = jnp.concatenate(
        [q_ref[...], ones8, jnp.zeros((DEEP - WIDE - 8, COLS), F32)], 0
    )
    returns = lax.dot(w_7[...], total, precision=lax.Precision.HIGHEST)
    lanes = lax.broadcasted_iota(jnp.int32, (1, 128), 1)
    rows16 = lax.broadcasted_iota(jnp.int32, (16, 128), 0)
    ones_row = jnp.where(lax.broadcasted_iota(jnp.int32, (32, CANDS_HERE), 0) == 0, 1.0, 0.0)
    out = []
    for e in range(ENVS_HERE):
        r = returns[0:1, e * CANDS_HERE : (e + 1) * CANDS_HERE]
        ret_ref[e : e + 1, :] = r
        lowest = jnp.min(r, axis=1, keepdims=True)
        highest = jnp.max(r, axis=1, keepdims=True)
        c = chosen[number, e : e + 1, :]
        w = c * (r - lowest + 1.0)
        hi, w1 = split(w)
        mid, w2 = split(w1)
        left = jnp.where(
            rows16 == 0,
            hi.astype(F32),
            jnp.where(rows16 == 1, mid.astype(F32), jnp.where(rows16 == 2, w2, jnp.where(rows16 == 3, c, 0.0))),
        ).astype(BF16)
        n = jnp.concatenate([noise[:, e * CANDS_HERE : (e + 1) * CANDS_HERE], ones_row], 0)
        n2_hi, n2_lo = split(n * n)
        right = jnp.concatenate([n.astype(BF16), n2_hi, n2_lo.astype(BF16)], 0)
        sums = lax.dot_general(left, right, (((1,), (1,)), ((), ())), preferred_element_type=F32)
        first_m, second_m = sums[:, :128], sums[:, 128:256] + sums[:, 256:]
        c1 = jnp.where(lanes == ONE + 1, highest, jnp.where(lanes == ONE + 2, lowest, first_m[3:4]))
        out += [
            first_m[0:1] + first_m[1:2] + first_m[2:3],
            c1,
            second_m[0:1] + second_m[1:2] + second_m[2:3],
            second_m[3:4],
        ]
    msg = jnp.concatenate(out, 0)
    for k in range(PEERS):
        msg_ref[k] = msg


def last_kernel(state_ref, got_ref, out_ref, best_ref):
    state, best = refit(state_ref[...], got_ref[...])
    out_ref[...] = jnp.transpose(state)
    best_ref[...] = best


VMEM = pl.BlockSpec(memory_space=pltpu.VMEM)


def rollout(number, weights, h0, z0, a_noise, s_noise, chosen, state, got):
    first = state is None
    shapes = [
        jax.ShapeDtypeStruct((ENVS_HERE, CANDS_HERE), F32),
        jax.ShapeDtypeStruct((PEERS, 8, 128), F32),
    ]
    args = [*weights, h0, z0, a_noise, s_noise, chosen]
    if not first:
        shapes += [
            jax.ShapeDtypeStruct((8, 128), F32),
            jax.ShapeDtypeStruct((ENVS_HERE, 128), F32),
        ]
        args += [state, got]
    return pl.pallas_call(
        functools.partial(rollout_kernel, first, number),
        out_shape=shapes,
        in_specs=[VMEM] * len(args),
        out_specs=[VMEM] * len(shapes),
        scratch_shapes=[
            pltpu.VMEM((ROWS, COLS), F32),
            pltpu.VMEM((WIDE, COLS), F32),
            pltpu.VMEM((WIDE, COLS), F32),
        ],
        compiler_params=pltpu.CompilerParams(vmem_limit_bytes=40 << 20),
        name=f"rollout_{number}",
    )(*args)


def prepared(flat):
    shapes = [(36, 200), (400, 400), (400, 200), (200, 200), (200, 60), (230, 200), (200, 1)]
    offset = 0
    mats, biases = [], []
    for fan_in, fan_out in shapes:
        mats.append(flat[offset : offset + fan_in * fan_out].reshape(fan_in, fan_out).T)
        offset += fan_in * fan_out
        b = flat[offset : offset + fan_out].astype(F32) * (bias_scale * fan_in**0.5)
        hi = b.astype(BF16)
        biases.append(jnp.stack([hi, (b - hi.astype(F32)).astype(BF16)], 1))
        offset += fan_out

    def pad(a, rows, cols):
        return jnp.pad(a, ((0, rows - a.shape[0]), (0, cols - a.shape[1])))

    def biased(a, b, rows=WIDE):
        return pad(jnp.concatenate([pad(a, a.shape[0], WIDE), b], 1), rows, DEEP)

    m1, m2, m3, m4, m5, m6, m7 = mats
    b1, b2, b3, b4, b5, b6, b7 = biases
    w_h = jnp.concatenate(
        [
            pad(m2[:200, 200:], WIDE, DEEP),
            pad(m2[200:, 200:], WIDE, DEEP),
            biased(m4, b4),
            biased(m6[:, :200], b6),
        ],
        0,
    )
    w_x = jnp.concatenate(
        [biased(m2[:200, :200], b2[:200]), biased(m2[200:, :200], b2[200:]), biased(m3[:, :200], b3)],
        0,
    )
    w_za = jnp.concatenate(
        [
            pad(jnp.concatenate([pad(m1[:, :30], 200, 32), pad(m1[:, 30:], 200, 8), b1], 1), WIDE, 48),
            pad(m6[:, 200:], WIDE, 48),
        ],
        0,
    )
    w_r = pad(m3[:, 200:], WIDE, DEEP)
    w_p = jnp.concatenate([biased(m5[:30], b5[:30], 32), biased(m5[30:], b5[30:], 32)], 0)
    last_bias = HOR * S200 * (b7[:, 0:1].astype(F32) + b7[:, 1:2].astype(F32))
    w_7 = pad(jnp.concatenate([pad(m7.astype(F32) * S200, 1, WIDE), last_bias], 1), 8, DEEP)
    return w_h, w_x, w_za, w_r, w_p, w_7


def from_peers(block, axis, peers, groups=None):
    return lax.all_to_all(
        jnp.broadcast_to(block[None], (peers, *block.shape)),
        axis,
        0,
        0,
        tiled=True,
        axis_index_groups=groups,
    )


def gathered_params(shard):
    size = shard.shape[0]
    block = jnp.pad(shard, (0, 2048 - size)).reshape(16, 128)
    block = from_peers(block, "env", 32)
    along_y = [[c, 2 + c, 4 + c, 6 + c] for c in range(2)]
    block = from_peers(block, "cand", 4, along_y)
    other = lax.ppermute(block, "cand", [(i, i ^ 1) for i in range(8)])
    low = lax.axis_index("cand") % 2 == 0
    both = jnp.stack([jnp.where(low, block, other), jnp.where(low, other, block)])
    both = both.reshape(2, 4, 32, 2048)[..., :size]
    return both.transpose(2, 1, 0, 3).reshape(-1)


def body(params, h_start, z_start, action_noise, state_noise, elites):
    a_noise = jnp.pad(
        action_noise.reshape(ITERS, HOR, ACT, COLS), ((0, 0), (0, 0), (0, 8 - ACT), (0, 0))
    ).reshape(ITERS, ROWS, COLS)
    s_noise = jnp.pad(
        state_noise.reshape(ITERS, HOR, STOCH, COLS), ((0, 0), (0, 0), (0, 32 - STOCH), (0, 0))
    )

    def spread_out(v, rows):
        v = jnp.pad(v.T, ((0, rows - v.shape[1]), (0, 0)))
        return jnp.broadcast_to(v[:, :, None], (rows, ENVS_HERE, CANDS_HERE)).reshape(rows, COLS)

    h0 = spread_out(h_start, WIDE)
    z0 = spread_out(z_start, 32)
    ids = lax.axis_index("cand") * CANDS_HERE + jnp.arange(CANDS_HERE, dtype=jnp.int32)
    chosen = jnp.any(elites[:, :, :, None] == ids, axis=2).astype(F32)

    weights = prepared(gathered_params(params))
    rets, bests = [], []
    state = got = None
    for number in range(ITERS):
        out = rollout(number, weights, h0, z0, a_noise, s_noise, chosen, state, got)
        rets.append(out[0])
        if number == 0:
            state = jnp.broadcast_to(
                jnp.array([0.0, 1.0, 0.0, 1.0, 0.0, 0.0, 0.0, 0.0], F32)[:, None], (8, 128)
            )
        else:
            state = out[2]
            bests.append(out[3])
        got = lax.all_to_all(out[1], "cand", 0, 0, tiled=True)
    columns, best = pl.pallas_call(
        last_kernel,
        out_shape=[
            jax.ShapeDtypeStruct((128, 8), F32),
            jax.ShapeDtypeStruct((ENVS_HERE, 128), F32),
        ],
        in_specs=[VMEM] * 2,
        out_specs=[VMEM] * 2,
        name="last",
    )(state, got)
    bests.append(best)
    columns = columns[:ROWS].reshape(HOR, 8, 8)[:, :ACT]
    return (
        columns[:, :, 0:4:2],
        columns[:, :, 1:4:2],
        jnp.stack(rets),
        jnp.stack([b[:, 0] for b in bests]),
    )


def solution(mesh):
    placed = (
        P(("env", "cand")),
        P("env", None),
        P("env", None),
        P(None, None, None, "env", "cand"),
        P(None, None, None, "env", "cand"),
        P(None, "env", None),
    )
    return jax.shard_map(
        body,
        mesh=mesh,
        in_specs=placed,
        out_specs=(
            P(None, None, "env"),
            P(None, None, "env"),
            P(None, "env", "cand"),
            P(None, "env"),
        ),
        check_vma=False,
    )
```

time: 196 us -> 127 us (0.65)
  matrix products: 55.7 us -> 0 us
  Pallas kernels: 0 us -> 46.9 us
  waiting for transfers between devices: 35.2 us -> 8.67 us
  starting transfers between devices: 34.9 us -> 11.4 us
  blocking collectives: 18.2 us -> 39.1 us
  other arithmetic: 17.8 us -> 3 us
  local copies, waits for them, and re-layouts: 29.9 us -> 15.7 us
    dot_general x180 -> x0, matrix products: 55.7 us -> none  [affine(): jnp.dot(matrix_t, inputs, preferred_element_type=jnp.float32) * factor]
    pallas_call x0 -> x4, Pallas kernels: none -> 46.9 us  [the longest x3 45.2 us: rollout(): pl.pallas_call(functools.partial(rollout_kernel, first, number), out_shap...]
    all_to_all x6 -> x2, starting transfers between devices: 34.9 us -> 7.93 us  [body(): got = lax.all_to_all(out[1], 'cand', 0, 0, tiled=True)]
    all_to_all x6 -> x2, waiting for transfers between devices: 35.2 us -> 8.66 us  [body(): got = lax.all_to_all(out[1], 'cand', 0, 0, tiled=True)]
    all_to_all x2 -> x3, blocking collectives: 18.2 us -> 39.1 us  [the longest x2 31.9 us: from_peers(): lax.all_to_all(jnp.broadcast_to(block[None], (peers, *block.shape)), axis...]
    squeeze x36 -> x0, local copies, waits for them, and re-layouts: 8.3 us -> none  [rollout(): final, _ = lax.scan(advance, initial, (action_seq, noise_seq))]
    broadcast_in_dim x1 -> x0, other arithmetic: 5 us -> none  [from_everyone(): jnp.broadcast_to(shard[None], (peers, *shard.shape))]
    all_to_all x2 -> x0, other arithmetic: 4.69 us -> none  [from_everyone(): lax.all_to_all(jnp.broadcast_to(shard[None], (peers, *shard.shape)), axis...]
  transfers between devices with their start and end apart: 6 -> 3, of which waited for: 6 -> 2; matrix products, arithmetic and copies ran while one was open for 3% -> 2% of each run, Pallas kernels for 0% -> 0%
where the time goes in v1:
time: 127 us
  Pallas kernels  46.9 us (37%)
  blocking collectives  39.1 us (31%)
  local copies, waits for them, and re-layouts  15.7 us (12%)
  starting transfers between devices  11.4 us (9%)
  waiting for transfers between devices  8.67 us (7%)
  other arithmetic  3 us (2%)
  between operations  1.79 us (1%)
    pallas_call x3, Pallas kernels, rollout(): pl.pallas_call(functools.partial(rollout_kernel, first, number), out_shap...  45.2 us
    all_to_all x2, blocking collectives, from_peers(): lax.all_to_all(jnp.broadcast_to(block[None], (peers, *block.shape)), axis...  31.9 us
    all_to_all x2, waiting for transfers between devices, body(): got = lax.all_to_all(out[1], 'cand', 0, 0, tiled=True)  8.66 us
    all_to_all x2, starting transfers between devices, body(): got = lax.all_to_all(out[1], 'cand', 0, 0, tiled=True)  7.93 us
    all_to_all x1, blocking collectives, body(): got = lax.all_to_all(out[1], 'cand', 0, 0, tiled=True)  7.25 us
    unnamed x31, local copies, waits for them, and re-layouts  4.48 us
    ppermute x1, starting transfers between devices, gathered_params(): other = lax.ppermute(block, 'cand', [(i, i ^ 1) for i in range(8)])  3.48 us
    reshape x11, local copies, waits for them, and re-layouts, prepared(): flat[offset:offset + fan_in * fan_out].reshape(fan_in, fan_out)  3.1 us
  transfers between devices with their start and end apart: 3, of which 2 were waited for; matrix products, arithmetic and copies ran while one was open for 2% of the time, Pallas kernels for 0%

profile of v1, /device:TPU:1, one launch (start us, length us, event | category | flops | bytes accessed | tf_op | source)
XLA Modules:
  0.0 126.6 jit_solution(3089944973628076395)
XLA Ops:
  0.6 0.7 pad_bitcast_fusion.1
  1.3 20.8 %all_to_all.25 = bf16[32,16,128]{2,1,0:T(8,128)(2,1)S(1)} all-to-all(bf16[32,16,128]{2,1,0:T(8,128)(2,1)S(1)} %broadcast_in_dim.13), channel_id=1, replica_groups=mesh['env'=32,'cand'=8] {'env'}, dimensions={0} | all-to-all | bytes 262144 | tf_op jit(solution)/shard_map/all_to_all | solution.py:259
  22.2 11.1 %all_to_all.26 = bf16[4,32,16,128]{3,2,1,0:T(8,128)(2,1)S(1)} all-to-all(bf16[4,32,16,128]{3,2,1,0:T(8,128)(2,1)S(1)} %broadcast_in_dim.14), channel_id=1, replica_groups={{0,2,4,6},{1,3,5,7},{8,10,12,14},{9,11,13,15},{16,18,20,22},{17,19,21,2..., dimensions={0} | all-to-all | bytes 1048576 | tf_op jit(solution)/shard_map/all_to_all | solution.py:259
  33.3 3.5 %collective-permute-start = (bf16[4,32,16,128]{3,2,1,0:T(8,128)(2,1)S(1)}, bf16[4,32,16,128]{3,2,1,0:T(8,128)(2,1)}, u32[]{:S(2)}, u32[]{:S(2)}) collective-permute-start(bf16[4,32,16,128]{3,2,1,0:T(8,128)(2,1)S(1)} %all_to_all.26), channel_id=1, source_target_pairs={{0,1},{1,0},{2,3},{3,2},{4,5},{5,4},{6,7},{7,6},{8,9},{9,8},{10,11... | collective-permute-start | bytes 1572872 | tf_op jit(solution)/shard_map/ppermute | solution.py:275
  36.8 0.2 compare_reduce_fusion
  37.0 0.4 reshape.80
  37.4 0.1 copy.114
  37.5 0.3 broadcast_in_dim.15
  37.8 0.4 copy-done.3
  38.7 1.1 broadcast_select_fusion.1
  39.8 0.2 stack.68
  40.0 0.2 stack.69
  40.3 0.7 copy.86
  41.1 0.8 reshape.69
  41.9 0.6 slice.182
  42.9 0.2 slice.155
  43.1 0.1 slice.168
  44.5 0.2 reshape.75
  45.0 0.1 copy.99
  45.1 0.4 reshape.72
  45.8 0.1 copy.107
  46.0 0.2 copy.108
  46.1 0.9 reshape.70
  47.0 0.2 copy.87
  47.2 0.1 fusion.61
  47.4 0.6 reshape.73
  48.0 0.1 copy.96
  48.7 0.3 reshape.71
  49.6 0.1 fusion.29
  49.9 14.4 %rollout_0.1 = (f32[2,128]{1,0:T(2,128)S(1)}, f32[8,8,128]{2,1,0:T(8,128)S(1)}) custom-call(bf16[832,256]{1,0:T(8,128)(2,1)S(1)} %fusion.10.w_h, bf16[624,256]{1,0:T(8,128)(2,1)S(1)} %fusion.13.w_x, bf16[416,48]{1,0:T(8,128)(2,1)S(1)} %fusion.26.w_za, bf16[208,256]{1,0:T(8,128)(2,1)S(1)} %pad.117.w_r, bf16[64,256]{1,0:T(8,128)(2,1)S(1)} %fusion.45.w_p, ...), custom_call_target="tpu_custom_call" | custom-call | tf_op jit(solution)/shard_map/rollout_0/pallas_call | solution.py:196
  64.3 7.3 %all_to_all.27.rest_1_ = f32[8,8,128]{2,1,0:T(8,128)S(1)} all-to-all(f32[8,8,128]{2,1,0:T(8,128)S(1)} %get-tuple-element.16), channel_id=1, replica_groups=mesh['env'=32,'cand'=8] {'cand'}, dimensions={0} | all-to-all | bytes 65536 | tf_op jit(solution)/shard_map/all_to_all | solution.py:312
  71.7 15.4 %rollout_1.1 = (f32[2,128]{1,0:T(2,128)S(1)}, f32[8,8,128]{2,1,0:T(8,128)}, f32[8,128]{1,0:T(8,128)S(1)}, f32[2,128]{1,0:T(2,128)S(1)}) custom-call(bf16[832,256]{1,0:T(8,128)(2,1)S(1)} %fusion.10.w_h, bf16[624,256]{1,0:T(8,128)(2,1)S(1)} %fusion.13.w_x, bf16[416,48]{1,0:T(8,128)(2,1)S(1)} %fusion.26.w_za, bf16[208,256]{1,0:T(8,128)(2,1)S(1)} %pad.117.w_r, ...), custom_call_target="tpu_custom_call" | custom-call | tf_op jit(solution)/shard_map/rollout_1/pallas_call | solution.py:196
  87.1 4.0 %all-to-all-start.3 = ((f32[8,8,128]{2,1,0:T(8,128)}), f32[8,8,128]{2,1,0:T(8,128)S(1)}, u32[]{:S(2)}, u32[]{:S(2)}) async-start(f32[8,8,128]{2,1,0:T(8,128)} %get-tuple-element.18), calls=%async_computation.3 | async-start | bytes 65536 | tf_op jit(solution)/shard_map/all_to_all | solution.py:312
  91.0 0.1 slice_reduce_fusion.2
  91.1 4.6 %all-to-all-done.3.rest_1_ = f32[8,8,128]{2,1,0:T(8,128)S(1)} async-done(((f32[8,8,128]{2,1,0:T(8,128)}), f32[8,8,128]{2,1,0:T(8,128)S(1)}, u32[]{:S(2)}, u32[]{:S(2)}) %all-to-all-start.3) | async-done | bytes 32800 | tf_op jit(solution)/shard_map/all_to_all | solution.py:312
  95.8 15.4 %rollout_2.1 = (f32[2,128]{1,0:T(2,128)S(1)}, f32[8,8,128]{2,1,0:T(8,128)}, f32[8,128]{1,0:T(8,128)S(1)}, f32[2,128]{1,0:T(2,128)S(1)}) custom-call(bf16[832,256]{1,0:T(8,128)(2,1)S(1)} %fusion.10.w_h, bf16[624,256]{1,0:T(8,128)(2,1)S(1)} %fusion.13.w_x, bf16[416,48]{1,0:T(8,128)(2,1)S(1)} %fusion.26.w_za, bf16[208,256]{1,0:T(8,128)(2,1)S(1)} %pad.117.w_r, ...), custom_call_target="tpu_custom_call" | custom-call | tf_op jit(solution)/shard_map/rollout_2/pallas_call | solution.py:196
  111.1 0.6 copy-done
  111.7 4.0 %all-to-all-start.4 = ((f32[8,8,128]{2,1,0:T(8,128)}), f32[8,8,128]{2,1,0:T(8,128)S(1)}, u32[]{:S(2)}, u32[]{:S(2)}) async-start(f32[8,8,128]{2,1,0:T(8,128)} %get-tuple-element.20), calls=%async_computation.4 | async-start | bytes 65536 | tf_op jit(solution)/shard_map/all_to_all | solution.py:312
  115.7 0.6 pad_maximum_fusion.1
  116.3 0.1 slice_reduce_fusion.1
  116.4 4.0 %all-to-all-done.4.got_ref = f32[8,8,128]{2,1,0:T(8,128)S(1)} async-done(((f32[8,8,128]{2,1,0:T(8,128)}), f32[8,8,128]{2,1,0:T(8,128)S(1)}, u32[]{:S(2)}, u32[]{:S(2)}) %all-to-all-start.4) | async-done | bytes 32800 | tf_op jit(solution)/shard_map/all_to_all | solution.py:312
  120.4 0.6 copy-done.2
  121.0 1.7 %last.1 = (f32[128,8]{1,0:T(8,128)}, f32[2,128]{1,0:T(2,128)}) custom-call(f32[8,128]{1,0:T(8,128)} %copy-done, f32[8,8,128]{2,1,0:T(8,128)} %copy-done.2), custom_call_target="tpu_custom_call" | custom-call | tf_op jit(solution)/shard_map/last/pallas_call | solution.py:313
  122.7 0.8 slice_bitcast_fusion
  123.7 0.8 slice_reduce_fusion
  124.5 0.7 copy.106
  125.2 0.7 copy.112
  125.9 0.7 copy.113
  (79 shorter events, 3.6 us)
Async XLA Ops:
  22.2 14.6 %copy-start.4 = (s32[3,2,100]{2,1,0:T(2,128)S(1)}, s32[3,2,100]{2,1,0:T(2,128)}, u32[]{:S(2)}) copy-start(s32[3,2,100]{2,1,0:T(2,128)} %param.12) | copy-start | bytes 7204
  22.2 14.8 %copy-start.1 = (bf16[3,12,30,2,128]{4,3,2,1,0:T(2,128)(2,1)S(1)}, bf16[3,12,30,2,128]{4,3,2,1,0:T(2,128)(2,1)}, u32[]{:S(2)}) copy-start(bf16[3,12,30,2,128]{4,3,2,1,0:T(2,128)(2,1)} %param.11) | copy-start | bytes 1658884
  33.3 4.1 %copy-start.5 = (f32[2,200]{1,0:T(2,128)S(1)}, f32[2,200]{1,0:T(2,128)}, u32[]{:S(2)}) copy-start(f32[2,200]{1,0:T(2,128)} %param.8) | copy-start | bytes 4804
  33.3 5.3 %collective-permute-start = (bf16[4,32,16,128]{3,2,1,0:T(8,128)(2,1)S(1)}, bf16[4,32,16,128]{3,2,1,0:T(8,128)(2,1)}, u32[]{:S(2)}, u32[]{:S(2)}) collective-permute-start(bf16[4,32,16,128]{3,2,1,0:T(8,128)(2,1)S(1)} %all_to_all.26), channel_id=1, source_target_pairs={{0,1},{1,0},{2,3},{3,2},{4,5},{5,4},{6,7},{7,6},{8,9},{9,8},{10,11... | collective-permute-start | bytes 1572872 | tf_op jit(solution)/shard_map/ppermute | solution.py:275
  37.4 0.9 copy-start.3
  37.4 1.0 copy-start.6
  42.9 2.0 %copy-start.8 = (pred[32]{0:T(512)(128)(4,1)S(1)}, pred[32]{0:T(512)(128)(4,1)}, u32[]{:S(2)}) copy-start(pred[32]{0:T(512)(128)(4,1)} %constant.42.clone.1) | copy-start | bytes 100
  47.2 1.0 copy-start.7
  49.9 21.7 %copy-start.9 = (f32[8]{0:T(128)S(1)}, f32[8]{0:T(128)}, u32[]{:S(2)}) copy-start(f32[8]{0:T(128)} %constant.50.clone) | copy-start | bytes 100
  87.1 8.7 %all-to-all-start.3 = ((f32[8,8,128]{2,1,0:T(8,128)}), f32[8,8,128]{2,1,0:T(8,128)S(1)}, u32[]{:S(2)}, u32[]{:S(2)}) async-start(f32[8,8,128]{2,1,0:T(8,128)} %get-tuple-element.18), calls=%async_computation.3 | async-start | bytes 65536 | tf_op jit(solution)/shard_map/all_to_all | solution.py:312
  111.1 0.6 copy-start
  111.7 8.7 %all-to-all-start.4 = ((f32[8,8,128]{2,1,0:T(8,128)}), f32[8,8,128]{2,1,0:T(8,128)S(1)}, u32[]{:S(2)}, u32[]{:S(2)}) async-start(f32[8,8,128]{2,1,0:T(8,128)} %get-tuple-element.20), calls=%async_computation.4 | async-start | bytes 65536 | tf_op jit(solution)/shard_map/all_to_all | solution.py:312
  120.4 0.6 copy-start.2

commit v2 on v1

v2 whole, which is shorter than its diff:
```python
import functools

import jax
import jax.numpy as jnp
from jax import lax
from jax.experimental import pallas as pl
from jax.experimental.pallas import tpu as pltpu
from jax.sharding import PartitionSpec as P

D_DET = 200
STOCH = 30
HID = 200
ACT = 6
HOR = 12
ITERS = 3

PEERS = 8
ENVS_HERE = 2
CANDS_HERE = 128
COLS = ENVS_HERE * CANDS_HERE

WIDE = 208
DEEP = 256
ROWS = 96
ONE = 96

bias_scale = 0.2
min_scale = 0.1
variance_floor = 1e-05

S36, S400, S200, S230 = (float(n) ** -0.5 for n in (36, 400, 200, 230))
LOG2E = 1.4426950408889634

F32, BF16 = jnp.float32, jnp.bfloat16


def dot(a, b):
    return jnp.dot(a, b, preferred_element_type=F32)


def scaled_elu(y, scale):
    return jnp.where(y > 0, y * scale, jnp.exp2(y * (scale * LOG2E)) - 1.0)


def softplus(v):
    return jnp.maximum(v, 0.0) + jnp.log(1.0 + jnp.exp(-jnp.abs(v)))


def refit(state, gathered):
    rows = []
    best = []
    for e in range(ENVS_HERE):
        m1, c1, m2, c2 = (gathered[:, 4 * e + k, :] for k in range(4))
        lowest = c1[:, ONE + 2 : ONE + 3]
        highest = c1[:, ONE + 1 : ONE + 2]
        worst = jnp.min(lowest, axis=0, keepdims=True)
        best.append(jnp.max(highest, axis=0, keepdims=True))
        lift = lowest - worst
        m1 = jnp.sum(m1 + lift * c1, axis=0, keepdims=True)
        m2 = jnp.sum(m2 + lift * c2, axis=0, keepdims=True)
        total = m1[:, ONE : ONE + 1]
        m1 = m1 / total
        m2 = m2 / total
        center = state[2 * e : 2 * e + 1]
        spread = state[2 * e + 1 : 2 * e + 2]
        rows.append(center + spread * m1)
        rows.append(
            jnp.sqrt(spread * spread * jnp.maximum(m2 - m1 * m1, 0.0) + variance_floor)
        )
    state = jnp.concatenate(rows + [jnp.zeros((4, 128), F32)], 0)
    return state, jnp.concatenate([jnp.broadcast_to(b, (1, 128)) for b in best], 0)


def split(v):
    hi = v.astype(BF16)
    return hi, v - hi.astype(F32)


def rollout_kernel(
    first, number, w_h, w_x, w_1, w_5, w_6z, w_r, w_7, h0, z0, a_noise, s_noise, chosen, *rest
):
    if first:
        ret_ref, msg_ref, acts = rest
    else:
        state_ref, got_ref, ret_ref, msg_ref, new_state_ref, best_ref, acts = rest
    noise = a_noise[number].astype(F32)
    if first:
        acts[...] = noise
    else:
        state, best = refit(state_ref[...], got_ref[...])
        new_state_ref[...] = state
        best_ref[...] = best
        columns = jnp.transpose(state)
        for e in range(ENVS_HERE):
            at = pl.ds(e * CANDS_HERE, CANDS_HERE)
            center = columns[:ROWS, 2 * e : 2 * e + 1]
            spread = columns[:ROWS, 2 * e + 1 : 2 * e + 2]
            acts[:, at] = center + spread * noise[:, e * CANDS_HERE : (e + 1) * CANDS_HERE]
    ones8 = jnp.where(lax.broadcasted_iota(jnp.int32, (8, COLS), 0) < 2, 1.0, 0.0).astype(F32)
    filler = jnp.zeros((80, COLS), F32)
    in_latent = lax.broadcasted_iota(jnp.int32, (1, 128), 1) < 32

    def drawn(t, n):
        block = jnp.concatenate([n, acts[t * 8 : t * 8 + 8, :], ones8, filler], 0)
        return jnp.transpose(block)

    def spread_out(ref):
        return jnp.concatenate(
            [jnp.broadcast_to(ref[e : e + 1, :], (CANDS_HERE, ref.shape[1])) for e in range(ENVS_HERE)], 0
        )

    h = spread_out(h0)
    q_sum = None
    for t in range(HOR + 1):
        hd = h.astype(BF16)
        if t == 0:
            za = (spread_out(z0) + drawn(0, jnp.zeros((32, COLS), F32))).astype(BF16)
        else:
            p = scaled_elu(dot(hd, w_h[:, 512:768]), S200).astype(BF16)
            s = dot(p, w_5[...]) * S200
            scale = jnp.where(in_latent, softplus(s[:, 128:]) + min_scale, 1.0)
            n = s_noise[number, t - 1].astype(F32)
            za = (s[:, :128] + scale * drawn(min(t, HOR - 1), n)).astype(BF16)
            q = scaled_elu(dot(hd, w_h[:, 768:]) + dot(za, w_6z[...]), S230)
            q = q.astype(BF16).astype(F32)
            q_sum = q if q_sum is None else q_sum + q
        if t == HOR:
            break
        x = scaled_elu(dot(za, w_1[...]), S36).astype(BF16)
        gates = dot(x, w_x[:, :512]) + dot(hd, w_h[:, :512])
        half = 0.5 * h
        rh = (half + jnp.tanh(gates[:, :256] * (0.5 * S400)) * half).astype(BF16)
        update = 0.5 + 0.5 * jnp.tanh(gates[:, 256:] * (0.5 * S400))
        proposal = jnp.tanh((dot(x, w_x[:, 512:]) + dot(rh, w_r[...])) * S400)
        h = proposal + update * (h - proposal)

    returns = lax.dot_general(
        w_7[...], q_sum, (((1,), (1,)), ((), ())), precision=lax.Precision.HIGHEST
    )
    lanes = lax.broadcasted_iota(jnp.int32, (1, 128), 1)
    rows16 = lax.broadcasted_iota(jnp.int32, (16, 128), 0)
    ones_row = jnp.where(lax.broadcasted_iota(jnp.int32, (32, CANDS_HERE), 0) == 0, 1.0, 0.0)
    out = []
    for e in range(ENVS_HERE):
        r = returns[0:1, e * CANDS_HERE : (e + 1) * CANDS_HERE]
        ret_ref[e : e + 1, :] = r
        lowest = jnp.min(r, axis=1, keepdims=True)
        highest = jnp.max(r, axis=1, keepdims=True)
        c = chosen[number, e : e + 1, :]
        w = c * (r - lowest + 1.0)
        hi, w1 = split(w)
        mid, w2 = split(w1)
        left = jnp.where(
            rows16 == 0,
            hi.astype(F32),
            jnp.where(rows16 == 1, mid.astype(F32), jnp.where(rows16 == 2, w2, jnp.where(rows16 == 3, c, 0.0))),
        ).astype(BF16)
        n = jnp.concatenate([noise[:, e * CANDS_HERE : (e + 1) * CANDS_HERE], ones_row], 0)
        n2_hi, n2_lo = split(n * n)
        right = jnp.concatenate([n.astype(BF16), n2_hi, n2_lo.astype(BF16)], 0)
        sums = lax.dot_general(left, right, (((1,), (1,)), ((), ())), preferred_element_type=F32)
        first_m, second_m = sums[:, :128], sums[:, 128:256] + sums[:, 256:]
        c1 = jnp.where(lanes == ONE + 1, highest, jnp.where(lanes == ONE + 2, lowest, first_m[3:4]))
        out += [
            first_m[0:1] + first_m[1:2] + first_m[2:3],
            c1,
            second_m[0:1] + second_m[1:2] + second_m[2:3],
            second_m[3:4],
        ]
    msg = jnp.concatenate(out, 0)
    for k in range(PEERS):
        msg_ref[k] = msg


def last_kernel(
    state_ref, got_ref, r0, r1, r2, b0, b1, mean_ref, spread_ref, ret_ref, best_ref
):
    state, best = refit(state_ref[...], got_ref[...])
    columns = jnp.transpose(state)
    lane = lax.broadcasted_iota(jnp.int32, (8, 128), 1)
    for e in range(ENVS_HERE):
        for ref, k in ((mean_ref, 2 * e), (spread_ref, 2 * e + 1)):
            table = jnp.zeros((8, 128), F32)
            for t in range(HOR):
                table = jnp.where(lane == t, columns[8 * t : 8 * t + 8, k : k + 1], table)
            for a in range(ACT):
                ref[a, e : e + 1, :] = table[a : a + 1, :HOR]
    for i, r in enumerate((r0, r1, r2)):
        ret_ref[i] = r[...]
    lane = lax.broadcasted_iota(jnp.int32, (ENVS_HERE, 128), 1)
    table = jnp.where(lane == 0, b0[...], jnp.where(lane == 1, b1[...], best))
    best_ref[...] = table[:, :ITERS]


VMEM = pl.BlockSpec(memory_space=pltpu.VMEM)


def rollout(number, weights, h0, z0, a_noise, s_noise, chosen, state, got):
    first = state is None
    shapes = [
        jax.ShapeDtypeStruct((ENVS_HERE, CANDS_HERE), F32),
        jax.ShapeDtypeStruct((PEERS, 8, 128), F32),
    ]
    args = [*weights, h0, z0, a_noise, s_noise, chosen]
    if not first:
        shapes += [
            jax.ShapeDtypeStruct((8, 128), F32),
            jax.ShapeDtypeStruct((ENVS_HERE, 128), F32),
        ]
        args += [state, got]
    return pl.pallas_call(
        functools.partial(rollout_kernel, first, number),
        out_shape=shapes,
        in_specs=[VMEM] * len(args),
        out_specs=[VMEM] * len(shapes),
        scratch_shapes=[pltpu.VMEM((ROWS, COLS), F32)],
        compiler_params=pltpu.CompilerParams(vmem_limit_bytes=40 << 20),
        name=f"rollout_{number}",
    )(*args)


PART = 1355
ROW = 200
TABLE = 1736


def prepare_kernel(own, other, w_h, w_x, w_1, w_5, w_6z, w_r, w_7, blocks, left, right, fifth_l, fifth_r):
    here = lax.axis_index("cand")
    y, core = here // 2, here % 2
    for k in range(4):
        there = (y // 2 ^ k // 2) * 2 + (y % 2 ^ k % 2)
        blocks[there * 2 + core] = own[k]
        blocks[there * 2 + 1 - core] = other[k]

    row = lax.broadcasted_iota(jnp.int32, (8, 128), 0)
    lane = lax.broadcasted_iota(jnp.int32, (8, 128), 1)
    for env in range(32):
        for cand in range(PEERS):
            start, first_lane = divmod(PART * (env * PEERS + cand), ROW)
            block = blocks[cand, env].astype(F32)
            for half, table in ((0, left), (1, right)):
                piece = block[:, 128 * half : 128 * half + 128]
                at = table.at[start : start + 8, :]
                if first_lane > 128 * half:
                    mask = (row > 0) | (lane >= first_lane - 128 * half)
                    pltpu.store(at, piece, mask=mask)
                else:
                    at[...] = piece

    def rows(start, count, step=1):
        at = pl.ds(start, count, stride=step) if step > 1 else pl.ds(start, count)
        return jnp.concatenate([left[at, :], right[at, :]], 1)

    row8 = lax.broadcasted_iota(jnp.int32, (8, 256), 0)
    lane8 = lax.broadcasted_iota(jnp.int32, (8, 256), 1)

    def foot(bias, fan_in, ones=0.0):
        bias = jnp.broadcast_to(bias * (bias_scale * fan_in**0.5), (8, 256))
        if ones:
            bias = jnp.where((lane8 == 200) | (lane8 == 201), ones, bias)
        hi = bias.astype(BF16).astype(F32)
        return jnp.where(row8 == 0, hi, jnp.where(row8 == 1, bias - hi, 0.0))

    def filled(parts, count=256):
        used = sum(part.shape[0] for part in parts)
        if used < count:
            parts = [*parts, jnp.zeros((count - used, 256), F32)]
        return jnp.concatenate(parts, 0).astype(BF16)

    first = rows(0, 37)
    state_rows = jnp.where(lax.broadcasted_iota(jnp.int32, (32, 256), 0) < STOCH, first[:32], 0.0)
    action_rows = jnp.where(row8 < ACT, rows(STOCH, 8), 0.0)
    w_1[...] = filled([state_rows, action_rows, foot(rows(36, 1), 36, 6.0)], 128)
    w_x[:, :256] = filled([rows(37, 200, 2), foot(rows(837, 1), 400)])
    w_x[:, 256:512] = filled([rows(38, 200, 2), foot(rows(838, 1), 400, 2000.0)])
    w_h[:, :256] = filled([rows(437, 200, 2)])
    w_h[:, 256:512] = filled([rows(438, 200, 2)])
    w_x[:, 512:] = filled([rows(839, 200), foot(rows(1239, 1), 400)])
    w_r[...] = filled([rows(1039, 200)])
    w_h[:, 512:768] = filled([rows(1240, 200), foot(rows(1440, 1), 200, 200**0.5)])

    def fifth(k, count):
        down, at = divmod(60 * k, ROW)
        piece = pltpu.roll(rows(1441 + down, count, 3), (256 - at) % 256, 1) if at else rows(1441 + down, count, 3)
        if at + 60 > ROW:
            more = pltpu.roll(rows(1442 + down, count, 3), ROW - at, 1)
            lanes = lax.broadcasted_iota(jnp.int32, (count, 256), 1)
            piece = jnp.where(lanes < ROW - at, piece, more)
        return piece

    def halves(piece):
        piece = piece[:, :128]
        lanes = lax.broadcasted_iota(jnp.int32, piece.shape, 1)
        return (
            jnp.where(lanes < STOCH, piece, 0.0),
            jnp.where(lanes < STOCH, pltpu.roll(piece, 128 - STOCH, 1), 0.0),
        )

    for k in range(10):
        mean, scale = halves(fifth(k, 20))
        fifth_l[pl.ds(k, 20, stride=10), :] = mean
        fifth_r[pl.ds(k, 20, stride=10), :] = scale
    last_row = rows(1501, 8)
    mean, scale = halves(last_row)
    bias = jnp.concatenate([mean, scale], 1)[0:1]
    w_5[...] = filled([jnp.concatenate([fifth_l[...], fifth_r[...]], 1), foot(bias, 200)])

    def shifted(start, count):
        one = pltpu.roll(rows(start, count), 256 - 60, 1)
        two = pltpu.roll(rows(start + 1, count), ROW - 60, 1)
        lanes = lax.broadcasted_iota(jnp.int32, (count, 256), 1)
        return jnp.where(lanes < ROW - 60, one, jnp.where(lanes < ROW, two, 0.0))

    w_h[:, 768:] = filled([shifted(1501, 200), foot(shifted(1731, 1), 230, 230**0.5)])
    below = shifted(1701, 32)
    below = jnp.where(lax.broadcasted_iota(jnp.int32, (32, 256), 0) < STOCH, below, 0.0)
    w_6z[...] = filled([below], 128)
    weight = shifted(1732, 1) * S200
    last_bias = pltpu.roll(rows(1733, 1), ROW - 60, 1) * bias_scale
    lanes = lax.broadcasted_iota(jnp.int32, (1, 256), 1)
    weight = jnp.where(lanes < ROW, weight, jnp.where(lanes == ROW, last_bias, 0.0))
    w_7[...] = jnp.broadcast_to(weight, (8, 256))


def prepared(own, other):
    return pl.pallas_call(
        prepare_kernel,
        out_shape=[
            jax.ShapeDtypeStruct((256, 1024), BF16),
            jax.ShapeDtypeStruct((256, 768), BF16),
            jax.ShapeDtypeStruct((128, 256), BF16),
            jax.ShapeDtypeStruct((256, 256), BF16),
            jax.ShapeDtypeStruct((128, 256), BF16),
            jax.ShapeDtypeStruct((256, 256), BF16),
            jax.ShapeDtypeStruct((8, 256), F32),
        ],
        in_specs=[VMEM] * 2,
        out_specs=[VMEM] * 7,
        scratch_shapes=[
            pltpu.VMEM((PEERS, 32, 8, 256), BF16),
            pltpu.VMEM((TABLE, 128), F32),
            pltpu.VMEM((TABLE, 128), F32),
            pltpu.VMEM((200, 128), F32),
            pltpu.VMEM((200, 128), F32),
        ],
        compiler_params=pltpu.CompilerParams(vmem_limit_bytes=40 << 20),
        name="prepare",
    )(own, other)


def gathered_params(shard):
    start = (lax.axis_index("env") * PEERS + lax.axis_index("cand")) * PART % ROW
    block = lax.dynamic_update_slice(jnp.zeros(8 * ROW, BF16), shard, (start,)).reshape(8, ROW)
    block = jnp.pad(block, ((0, 0), (0, 256 - ROW)))
    block = lax.all_to_all(jnp.broadcast_to(block[None], (32, 8, 256)), "env", 0, 0, tiled=True)
    near = [lax.ppermute(block, "cand", [(i, i ^ 2 * k) for i in range(PEERS)]) for k in (1, 2, 3)]
    own = jnp.stack([block, *near])
    return own, lax.ppermute(own, "cand", [(i, i ^ 1) for i in range(PEERS)])


def body(params, h_start, z_start, action_noise, state_noise, elites):
    a_noise = jnp.pad(
        action_noise.reshape(ITERS, HOR, ACT, COLS), ((0, 0), (0, 0), (0, 8 - ACT), (0, 0))
    ).reshape(ITERS, ROWS, COLS)
    s_noise = jnp.pad(
        state_noise.reshape(ITERS, HOR, STOCH, COLS), ((0, 0), (0, 0), (0, 32 - STOCH), (0, 0))
    )

    h0 = jnp.concatenate(
        [h_start, jnp.ones((ENVS_HERE, 2), F32), jnp.zeros((ENVS_HERE, 54), F32)], 1
    )
    z0 = jnp.pad(z_start, ((0, 0), (0, 128 - STOCH)))
    ids = lax.axis_index("cand") * CANDS_HERE + jnp.arange(CANDS_HERE, dtype=jnp.int32)
    chosen = jnp.any(elites[:, :, :, None] == ids, axis=2).astype(F32)

    weights = prepared(*gathered_params(params))
    rets, bests = [], []
    state = got = None
    for number in range(ITERS):
        out = rollout(number, weights, h0, z0, a_noise, s_noise, chosen, state, got)
        rets.append(out[0])
        if number == 0:
            state = jnp.broadcast_to(
                jnp.array([0.0, 1.0, 0.0, 1.0, 0.0, 0.0, 0.0, 0.0], F32)[:, None], (8, 128)
            )
        else:
            state = out[2]
            bests.append(out[3])
        got = lax.all_to_all(out[1], "cand", 0, 0, tiled=True)
    mean, spread, returns, best = pl.pallas_call(
        last_kernel,
        out_shape=[
            jax.ShapeDtypeStruct((ACT, ENVS_HERE, HOR), F32),
            jax.ShapeDtypeStruct((ACT, ENVS_HERE, HOR), F32),
            jax.ShapeDtypeStruct((ITERS, ENVS_HERE, CANDS_HERE), F32),
            jax.ShapeDtypeStruct((ENVS_HERE, ITERS), F32),
        ],
        in_specs=[VMEM] * 7,
        out_specs=[VMEM] * 4,
        name="last",
    )(state, got, *rets, *bests)
    return mean.transpose(2, 0, 1), spread.transpose(2, 0, 1), returns, best.T


def solution(mesh):
    placed = (
        P(("env", "cand")),
        P("env", None),
        P("env", None),
        P(None, None, None, "env", "cand"),
        P(None, None, None, "env", "cand"),
        P(None, "env", None),
    )
    return jax.shard_map(
        body,
        mesh=mesh,
        in_specs=placed,
        out_specs=(
            P(None, None, "env"),
            P(None, None, "env"),
            P(None, "env", "cand"),
            P(None, "env"),
        ),
        check_vma=False,
    )
```

time: 127 us -> 97.8 us (0.77)
  Pallas kernels: 46.9 us -> 34.3 us
  local copies, waits for them, and re-layouts: 15.7 us -> 4.4 us
  blocking collectives: 39.1 us -> 44.7 us
  starting transfers between devices: 11.4 us -> 7.49 us
  waiting for transfers between devices: 8.67 us -> 5.5 us
  other arithmetic: 3 us -> 0.25 us
    all_to_all x1 -> x3, blocking collectives: 7.25 us -> 23.9 us  [body(): got = lax.all_to_all(out[1], 'cand', 0, 0, tiled=True)]
    pallas_call x3, Pallas kernels: 45.2 us -> 31.9 us  [rollout(): pl.pallas_call(functools.partial(rollout_kernel, first, number), out_shap...]
    all_to_all x2 -> x1, blocking collectives: 31.9 us -> 20.8 us  [gathered_params(): lax.all_to_all(jnp.broadcast_to(block[None], (32, 8, 256)), 'env', 0, 0,...]
    all_to_all x2 -> x0, waiting for transfers between devices: 8.66 us -> none  [body(): got = lax.all_to_all(out[1], 'cand', 0, 0, tiled=True)]
    all_to_all x2 -> x0, starting transfers between devices: 7.93 us -> none  [body(): got = lax.all_to_all(out[1], 'cand', 0, 0, tiled=True)]
    ppermute x1 -> x4, waiting for transfers between devices: 0.01 us -> 5.5 us  [the longest x3 5.5 us: gathered_params(): lax.ppermute(block, 'cand', [(i, i ^ 2 * k) for i in range(PEERS)])]
    reshape x13 -> x1, local copies, waits for them, and re-layouts: 4.72 us -> 0.09 us  [gathered_params(): lax.dynamic_update_slice(jnp.zeros(8 * ROW, BF16), shard, (start,))]
    ppermute x1 -> x4, starting transfers between devices: 3.48 us -> 7.49 us  [the longest x3 3.92 us: gathered_params(): lax.ppermute(block, 'cand', [(i, i ^ 2 * k) for i in range(PEERS)])]
  transfers between devices with their start and end apart: 3 -> 4, of which waited for: 2 -> 2; matrix products, arithmetic and copies ran while one was open for 2% -> 1% of each run, Pallas kernels for 0% -> 0%
where the time goes in v2:
time: 97.8 us; the launch traced here: 97.4 us
  blocking collectives  44.7 us (46%)
  Pallas kernels  34.3 us (35%)
  starting transfers between devices  7.49 us (8%)
  waiting for transfers between devices  5.5 us (6%)
  local copies, waits for them, and re-layouts  4.4 us (4%)
    pallas_call x3, Pallas kernels, rollout(): pl.pallas_call(functools.partial(rollout_kernel, first, number), out_shap...  31.9 us
    all_to_all x3, blocking collectives, body(): got = lax.all_to_all(out[1], 'cand', 0, 0, tiled=True)  23.9 us
    all_to_all x1, blocking collectives, gathered_params(): lax.all_to_all(jnp.broadcast_to(block[None], (32, 8, 256)), 'env', 0, 0,...  20.8 us
    ppermute x3, waiting for transfers between devices, gathered_params(): lax.ppermute(block, 'cand', [(i, i ^ 2 * k) for i in range(PEERS)])  5.5 us
    ppermute x3, starting transfers between devices, gathered_params(): lax.ppermute(block, 'cand', [(i, i ^ 2 * k) for i in range(PEERS)])  3.92 us
    ppermute x1, starting transfers between devices, gathered_params(): return (own, lax.ppermute(own, 'cand', [(i, i ^ 1) for i in range(PEERS)]))  3.57 us
    unnamed x26, local copies, waits for them, and re-layouts  3.37 us
  transfers between devices with their start and end apart: 4, of which 2 were waited for; matrix products, arithmetic and copies ran while one was open for 1% of the time, Pallas kernels for 0%

profile of v2, /device:TPU:1, one launch (start us, length us, event | category | flops | bytes accessed | tf_op | source)
XLA Modules:
  0.0 97.4 jit_solution(13710617053994579898)
XLA Ops:
  0.7 0.0 copy-start.8
  0.7 0.7 copy-done.8
  1.3 0.2 dynamic_update_slice.3
  1.5 0.1 reshape.27
  1.6 20.8 %all_to_all.20 = bf16[32,8,256]{2,1,0:T(8,128)(2,1)S(1)} all-to-all(bf16[32,8,256]{2,1,0:T(8,128)(2,1)S(1)} %broadcast_in_dim.9), channel_id=1, replica_groups=mesh['env'=32,'cand'=8] {'env'}, dimensions={0} | all-to-all | bytes 262144 | tf_op jit(solution)/shard_map/all_to_all | solution.py:355
  22.5 0.0 copy-start.6
  22.5 1.3 %collective-permute-start = (bf16[32,8,256]{2,1,0:T(8,128)(2,1)S(1)}, bf16[32,8,256]{2,1,0:T(8,128)(2,1)S(1)}, u32[]{:S(2)}, u32[]{:S(2)}) collective-permute-start(bf16[32,8,256]{2,1,0:T(8,128)(2,1)S(1)} %all_to_all.20), channel_id=1, source_target_pairs={{0,2},{1,3},{2,0},{3,1},{4,6},{5,7},{6,4},{7,5},{8,10},{9,11},{10,... | collective-permute-start | bytes 393224 | tf_op jit(solution)/shard_map/ppermute | solution.py:356
  23.8 2.6 %collective-permute-start.1 = (bf16[32,8,256]{2,1,0:T(8,128)(2,1)S(1)}, bf16[32,8,256]{2,1,0:T(8,128)(2,1)S(1)}, u32[]{:S(2)}, u32[]{:S(2)}) collective-permute-start(bf16[32,8,256]{2,1,0:T(8,128)(2,1)S(1)} %all_to_all.20), channel_id=1, source_target_pairs={{0,4},{1,5},{2,6},{3,7},{4,0},{5,1},{6,2},{7,3},{8,12},{9,13},{10,... | collective-permute-start | bytes 393224 | tf_op jit(solution)/shard_map/ppermute | solution.py:356
  26.4 0.0 collective-permute-start.2
  26.4 0.0 collective-permute-done
  26.4 4.0 %collective-permute-done.1 = bf16[32,8,256]{2,1,0:T(8,128)(2,1)S(1)} collective-permute-done((bf16[32,8,256]{2,1,0:T(8,128)(2,1)S(1)}, bf16[32,8,256]{2,1,0:T(8,128)(2,1)S(1)}, u32[]{:S(2)}, u32[]{:S(2)}) %collective-permute-start.1) | collective-permute-done | bytes 131104 | tf_op jit(solution)/shard_map/ppermute | solution.py:356
  30.3 1.5 %collective-permute-done.2 = bf16[32,8,256]{2,1,0:T(8,128)(2,1)S(1)} collective-permute-done((bf16[32,8,256]{2,1,0:T(8,128)(2,1)S(1)}, bf16[32,8,256]{2,1,0:T(8,128)(2,1)S(1)}, u32[]{:S(2)}, u32[]{:S(2)}) %collective-permute-start.2) | collective-permute-done | bytes 131104 | tf_op jit(solution)/shard_map/ppermute | solution.py:356
  31.9 0.0 copy-start.9
  31.9 0.1 pad_maximum_fusion.own
  32.0 3.6 %collective-permute-start.3 = (bf16[4,32,8,256]{3,2,1,0:T(8,128)(2,1)S(1)}, bf16[4,32,8,256]{3,2,1,0:T(8,128)(2,1)S(1)}, u32[]{:S(2)}, u32[]{:S(2)}) collective-permute-start(bf16[4,32,8,256]{3,2,1,0:T(8,128)(2,1)S(1)} %pad_maximum_fusion.own), channel_id=1, source_target_pairs={{0,1},{1,0},{2,3},{3,2},{4,5},{5,4},{6,7},{7,6},{8,9},{9,8},{10,11... | collective-permute-start | bytes 1572872 | tf_op jit(solution)/shard_map/ppermute | solution.py:358
  35.5 0.0 copy-done.9
  35.5 0.2 compare_reduce_fusion
  35.7 0.0 copy-done.6
  35.7 0.4 reshape.30
  36.1 0.0 copy-start.7
  36.1 0.1 pad.19.s_noise
  36.2 0.8 copy-done.7
  37.0 0.1 reshape.28
  37.1 0.1 pad.21.clone
  37.2 0.0 copy-start.11
  37.2 0.1 pad.22.clone
  37.2 0.6 copy-done.11
  37.9 0.6 copy-done.10
  38.5 0.0 collective-permute-done.3.other
  38.5 0.6 prepare.1
  39.1 10.3 %rollout_0.1 = (f32[2,128]{1,0:T(2,128)S(1)}, f32[8,8,128]{2,1,0:T(8,128)S(1)}) custom-call(bf16[256,1024]{1,0:T(8,128)(2,1)S(1)} %get-tuple-element.25.w_h, bf16[256,768]{1,0:T(8,128)(2,1)S(1)} %get-tuple-element.26.w_x, bf16[128,256]{1,0:T(8,128)(2,1)S(1)} %get-tuple-element.27.w_1, bf16[256,256]{1,0:T(8,128)(2,1)S(1)} %get-tuple-element.28.w_5, ...), custom_call_target="tpu_custom_call" | custom-call | tf_op jit(solution)/shard_map/rollout_0/pallas_call | solution.py:211
  49.4 0.6 copy-done.1
  50.0 7.5 %all_to_all.21.rest_1_ = f32[8,8,128]{2,1,0:T(8,128)S(1)} all-to-all(f32[8,8,128]{2,1,0:T(8,128)S(1)} %get-tuple-element.32), channel_id=1, replica_groups=mesh['env'=32,'cand'=8] {'cand'}, dimensions={0} | all-to-all | bytes 65536 | tf_op jit(solution)/shard_map/all_to_all | solution.py:389
  57.5 0.0 copy-done.12
  57.5 0.1 broadcast_in_dim.11.rest_0_
  57.6 10.8 %rollout_1.1 = (f32[2,128]{1,0:T(2,128)S(1)}, f32[8,8,128]{2,1,0:T(8,128)S(1)}, f32[8,128]{1,0:T(8,128)S(1)}, f32[2,128]{1,0:T(2,128)S(1)}) custom-call(bf16[256,1024]{1,0:T(8,128)(2,1)S(1)} %get-tuple-element.25.w_h, bf16[256,768]{1,0:T(8,128)(2,1)S(1)} %get-tuple-element.26.w_x, bf16[128,256]{1,0:T(8,128)(2,1)S(1)} %get-tuple-element.27.w_1, ...), custom_call_target="tpu_custom_call" | custom-call | tf_op jit(solution)/shard_map/rollout_1/pallas_call | solution.py:211
  68.4 0.0 copy-start.3
  68.4 7.8 %all_to_all.22.rest_1_ = f32[8,8,128]{2,1,0:T(8,128)S(1)} all-to-all(f32[8,8,128]{2,1,0:T(8,128)S(1)} %get-tuple-element.34), channel_id=1, replica_groups=mesh['env'=32,'cand'=8] {'cand'}, dimensions={0} | all-to-all | bytes 65536 | tf_op jit(solution)/shard_map/all_to_all | solution.py:389
  76.3 0.0 copy-done.2
  76.3 0.0 copy-done.3
  76.3 10.8 %rollout_2.1 = (f32[2,128]{1,0:T(2,128)S(1)}, f32[8,8,128]{2,1,0:T(8,128)S(1)}, f32[8,128]{1,0:T(8,128)S(1)}, f32[2,128]{1,0:T(2,128)S(1)}) custom-call(bf16[256,1024]{1,0:T(8,128)(2,1)S(1)} %get-tuple-element.25.w_h, bf16[256,768]{1,0:T(8,128)(2,1)S(1)} %get-tuple-element.26.w_x, bf16[128,256]{1,0:T(8,128)(2,1)S(1)} %get-tuple-element.27.w_1, ...), custom_call_target="tpu_custom_call" | custom-call | tf_op jit(solution)/shard_map/rollout_2/pallas_call | solution.py:211
  87.1 0.0 copy-start.4
  87.1 0.0 copy-start.5
  87.1 8.5 %all_to_all.23.got_ref = f32[8,8,128]{2,1,0:T(8,128)} all-to-all(f32[8,8,128]{2,1,0:T(8,128)S(1)} %get-tuple-element.36), channel_id=1, replica_groups=mesh['env'=32,'cand'=8] {'cand'}, dimensions={0} | all-to-all | bytes 65536 | tf_op jit(solution)/shard_map/all_to_all | solution.py:389
  95.6 0.0 copy-done
  95.6 0.0 copy-done.4
  95.6 0.0 copy-done.5
  95.6 1.8 %last.1 = (f32[6,2,12]{2,1,0:T(2,128)}, f32[6,2,12]{2,1,0:T(2,128)}, f32[3,2,128]{2,1,0:T(2,128)}, f32[2,3]{1,0:T(2,128)}) custom-call(f32[8,128]{1,0:T(8,128)} %copy-done, f32[8,8,128]{2,1,0:T(8,128)} %all_to_all.23.got_ref, f32[2,128]{1,0:T(2,128)} %copy-done.1, f32[2,128]{1,0:T(2,128)} %copy-done.2, f32[2,128]{1,0:T(2,128)} %copy-done.4, ...), custom_call_target="tpu_custom_call" | custom-call | tf_op jit(solution)/shard_map/last/pallas_call | solution.py:390
  (15 shorter events, 0.1 us)
Async XLA Ops:
  0.7 0.7 copy-start.8
  22.5 13.3 %copy-start.6 = (bf16[3,12,30,2,128]{4,3,2,1,0:T(2,128)(2,1)S(1)}, bf16[3,12,30,2,128]{4,3,2,1,0:T(2,128)(2,1)}, u32[]{:S(2)}) copy-start(bf16[3,12,30,2,128]{4,3,2,1,0:T(2,128)(2,1)} %param.11) | copy-start | bytes 1658884
  22.5 3.9 %collective-permute-start = (bf16[32,8,256]{2,1,0:T(8,128)(2,1)S(1)}, bf16[32,8,256]{2,1,0:T(8,128)(2,1)S(1)}, u32[]{:S(2)}, u32[]{:S(2)}) collective-permute-start(bf16[32,8,256]{2,1,0:T(8,128)(2,1)S(1)} %all_to_all.20), channel_id=1, source_target_pairs={{0,2},{1,3},{2,0},{3,1},{4,6},{5,7},{6,4},{7,5},{8,10},{9,11},{10,... | collective-permute-start | bytes 393224 | tf_op jit(solution)/shard_map/ppermute | solution.py:356
  23.8 6.6 %collective-permute-start.1 = (bf16[32,8,256]{2,1,0:T(8,128)(2,1)S(1)}, bf16[32,8,256]{2,1,0:T(8,128)(2,1)S(1)}, u32[]{:S(2)}, u32[]{:S(2)}) collective-permute-start(bf16[32,8,256]{2,1,0:T(8,128)(2,1)S(1)} %all_to_all.20), channel_id=1, source_target_pairs={{0,4},{1,5},{2,6},{3,7},{4,0},{5,1},{6,2},{7,3},{8,12},{9,13},{10,... | collective-permute-start | bytes 393224 | tf_op jit(solution)/shard_map/ppermute | solution.py:356
  26.4 5.5 %collective-permute-start.2 = (bf16[32,8,256]{2,1,0:T(8,128)(2,1)S(1)}, bf16[32,8,256]{2,1,0:T(8,128)(2,1)S(1)}, u32[]{:S(2)}, u32[]{:S(2)}) collective-permute-start(bf16[32,8,256]{2,1,0:T(8,128)(2,1)S(1)} %all_to_all.20), channel_id=1, source_target_pairs={{0,6},{1,7},{2,4},{3,5},{4,2},{5,3},{6,0},{7,1},{8,14},{9,15},{10,... | collective-permute-start | bytes 393224 | tf_op jit(solution)/shard_map/ppermute | solution.py:356
  31.9 3.7 %copy-start.9 = (s32[3,2,100]{2,1,0:T(2,128)S(1)}, s32[3,2,100]{2,1,0:T(2,128)}, u32[]{:S(2)}) copy-start(s32[3,2,100]{2,1,0:T(2,128)} %param.12) | copy-start | bytes 7204
  32.0 6.6 %collective-permute-start.3 = (bf16[4,32,8,256]{3,2,1,0:T(8,128)(2,1)S(1)}, bf16[4,32,8,256]{3,2,1,0:T(8,128)(2,1)S(1)}, u32[]{:S(2)}, u32[]{:S(2)}) collective-permute-start(bf16[4,32,8,256]{3,2,1,0:T(8,128)(2,1)S(1)} %pad_maximum_fusion.own), channel_id=1, source_target_pairs={{0,1},{1,0},{2,3},{3,2},{4,5},{5,4},{6,7},{7,6},{8,9},{9,8},{10,11... | collective-permute-start | bytes 1572872 | tf_op jit(solution)/shard_map/ppermute | solution.py:358
  36.1 0.9 copy-start.7
  37.2 0.7 copy-start.11
  37.8 0.7 copy-start.10
  49.4 0.6 copy-start.1
  50.0 7.5 %copy-start.12 = (f32[8]{0:T(128)S(1)}, f32[8]{0:T(128)}, u32[]{:S(2)}) copy-start(f32[8]{0:T(128)} %constant.40.clone) | copy-start | bytes 100
  68.4 7.8 %copy-start.2 = (f32[2,128]{1,0:T(2,128)}, f32[2,128]{1,0:T(2,128)S(1)}, u32[]{:S(2)}) copy-start(f32[2,128]{1,0:T(2,128)S(1)} %get-tuple-element.38.r1) | copy-start | bytes 3076
  68.4 7.8 %copy-start.3 = (f32[2,128]{1,0:T(2,128)}, f32[2,128]{1,0:T(2,128)S(1)}, u32[]{:S(2)}) copy-start(f32[2,128]{1,0:T(2,128)S(1)} %get-tuple-element.40.b0) | copy-start | bytes 3076
  87.1 8.5 %copy-start = (f32[8,128]{1,0:T(8,128)}, f32[8,128]{1,0:T(8,128)S(1)}, u32[]{:S(2)}) copy-start(f32[8,128]{1,0:T(8,128)S(1)} %get-tuple-element.35.state_ref) | copy-start | bytes 12292
  87.1 8.5 %copy-start.4 = (f32[2,128]{1,0:T(2,128)}, f32[2,128]{1,0:T(2,128)S(1)}, u32[]{:S(2)}) copy-start(f32[2,128]{1,0:T(2,128)S(1)} %get-tuple-element.39.r2) | copy-start | bytes 3076
  87.1 8.5 %copy-start.5 = (f32[2,128]{1,0:T(2,128)}, f32[2,128]{1,0:T(2,128)S(1)}, u32[]{:S(2)}) copy-start(f32[2,128]{1,0:T(2,128)S(1)} %get-tuple-element.41.b1) | copy-start | bytes 3076

commit v3 on v2

--- a/solution.py
+++ b/solution.py
@@ -36,6 +36,10 @@
 
 def dot(a, b):
     return jnp.dot(a, b, preferred_element_type=F32)
+
+
+def dot_t(a, b):
+    return lax.dot_general(a, b, (((1,), (1,)), ((), ())), preferred_element_type=F32)
 
 
 def scaled_elu(y, scale):
@@ -134,38 +138,48 @@
         proposal = jnp.tanh((dot(x, w_x[:, 512:]) + dot(rh, w_r[...])) * S400)
         h = proposal + update * (h - proposal)
 
-    returns = lax.dot_general(
-        w_7[...], q_sum, (((1,), (1,)), ((), ())), precision=lax.Precision.HIGHEST
-    )
+    wide = lax.broadcasted_iota(jnp.int32, (1, COLS), 1)
+    wide16 = lax.broadcasted_iota(jnp.int32, (16, COLS), 1) // CANDS_HERE
+    rows16 = lax.broadcasted_iota(jnp.int32, (16, COLS), 0)
     lanes = lax.broadcasted_iota(jnp.int32, (1, 128), 1)
-    rows16 = lax.broadcasted_iota(jnp.int32, (16, 128), 0)
-    ones_row = jnp.where(lax.broadcasted_iota(jnp.int32, (32, CANDS_HERE), 0) == 0, 1.0, 0.0)
+
+    weight = jnp.where(rows16 == 0, w_7[0:1, :], 0.0).astype(BF16)
+    part_1, left_over = split(q_sum)
+    part_2, left_over = split(left_over)
+    r = dot_t(weight, part_1) + (dot_t(weight, part_2) + dot_t(weight, left_over.astype(BF16)))
+    n = jnp.concatenate(
+        [noise, jnp.where(lax.broadcasted_iota(jnp.int32, (32, COLS), 0) == 0, 1.0, 0.0)], 0
+    )
+    n2_hi, n2_lo = split(n * n)
+    r = r[0:1] * S200 + w_7[1:2, :]
+    ends = []
+    for e in range(ENVS_HERE):
+        mine = r[:, e * CANDS_HERE : (e + 1) * CANDS_HERE]
+        ret_ref[e : e + 1, :] = mine
+        ends.append((jnp.min(mine, axis=1, keepdims=True), jnp.max(mine, axis=1, keepdims=True)))
+    lowest = jnp.where(wide < CANDS_HERE, ends[0][0], ends[1][0])
+    c = jnp.concatenate([chosen[number, e : e + 1, :] for e in range(ENVS_HERE)], 1)
+    w = c * (r - lowest + 1.0)
+    hi, w1 = split(w)
+    mid, w2 = split(w1)
+    kind = rows16 % 4
+    left = jnp.where(
+        kind == 0, hi.astype(F32), jnp.where(kind == 1, mid.astype(F32), jnp.where(kind == 2, w2, c))
+    )
+    left = jnp.where(rows16 // 4 == wide16, left, 0.0).astype(BF16)
+    sums = dot_t(left, jnp.concatenate([n.astype(BF16), n2_hi, n2_lo.astype(BF16)], 0))
+    first_m, second_m = sums[:8, :128], sums[:8, 128:256] + sums[:8, 256:]
     out = []
     for e in range(ENVS_HERE):
-        r = returns[0:1, e * CANDS_HERE : (e + 1) * CANDS_HERE]
-        ret_ref[e : e + 1, :] = r
-        lowest = jnp.min(r, axis=1, keepdims=True)
-        highest = jnp.max(r, axis=1, keepdims=True)
-        c = chosen[number, e : e + 1, :]
-        w = c * (r - lowest + 1.0)
-        hi, w1 = split(w)
-        mid, w2 = split(w1)
-        left = jnp.where(
-            rows16 == 0,
-            hi.astype(F32),
-            jnp.where(rows16 == 1, mid.astype(F32), jnp.where(rows16 == 2, w2, jnp.where(rows16 == 3, c, 0.0))),
-        ).astype(BF16)
-        n = jnp.concatenate([noise[:, e * CANDS_HERE : (e + 1) * CANDS_HERE], ones_row], 0)
-        n2_hi, n2_lo = split(n * n)
-        right = jnp.concatenate([n.astype(BF16), n2_hi, n2_lo.astype(BF16)], 0)
-        sums = lax.dot_general(left, right, (((1,), (1,)), ((), ())), preferred_element_type=F32)
-        first_m, second_m = sums[:, :128], sums[:, 128:256] + sums[:, 256:]
-        c1 = jnp.where(lanes == ONE + 1, highest, jnp.where(lanes == ONE + 2, lowest, first_m[3:4]))
+        k = 4 * e
+        lowest, highest = ends[e]
         out += [
-            first_m[0:1] + first_m[1:2] + first_m[2:3],
-            c1,
-            second_m[0:1] + second_m[1:2] + second_m[2:3],
-            second_m[3:4],
+            first_m[k : k + 1] + first_m[k + 1 : k + 2] + first_m[k + 2 : k + 3],
+            jnp.where(
+                lanes == ONE + 1, highest, jnp.where(lanes == ONE + 2, lowest, first_m[k + 3 : k + 4])
+            ),
+            second_m[k : k + 1] + second_m[k + 1 : k + 2] + second_m[k + 2 : k + 3],
+            second_m[k + 3 : k + 4],
         ]
     msg = jnp.concatenate(out, 0)
     for k in range(PEERS):
@@ -315,11 +329,8 @@
     below = shifted(1701, 32)
     below = jnp.where(lax.broadcasted_iota(jnp.int32, (32, 256), 0) < STOCH, below, 0.0)
     w_6z[...] = filled([below], 128)
-    weight = shifted(1732, 1) * S200
-    last_bias = pltpu.roll(rows(1733, 1), ROW - 60, 1) * bias_scale
-    lanes = lax.broadcasted_iota(jnp.int32, (1, 256), 1)
-    weight = jnp.where(lanes < ROW, weight, jnp.where(lanes == ROW, last_bias, 0.0))
-    w_7[...] = jnp.broadcast_to(weight, (8, 256))
+    last_bias = left[1733:1734, 60:61] * (HOR * bias_scale)
+    w_7[...] = jnp.where(row8 == 0, shifted(1732, 1), last_bias)
 
 
 def prepared(own, other):
@@ -348,17 +359,19 @@
     )(own, other)
 
 
-def gathered_params(shard):
+def from_env(shard):
     start = (lax.axis_index("env") * PEERS + lax.axis_index("cand")) * PART % ROW
     block = lax.dynamic_update_slice(jnp.zeros(8 * ROW, BF16), shard, (start,)).reshape(8, ROW)
     block = jnp.pad(block, ((0, 0), (0, 256 - ROW)))
-    block = lax.all_to_all(jnp.broadcast_to(block[None], (32, 8, 256)), "env", 0, 0, tiled=True)
+    return lax.all_to_all(jnp.broadcast_to(block[None], (32, 8, 256)), "env", 0, 0, tiled=True)
+
+
+def body(params, h_start, z_start, action_noise, state_noise, elites):
+    block = from_env(params)
+    block, h_start, z_start, action_noise, state_noise, elites = lax.optimization_barrier(
+        (block, h_start, z_start, action_noise, state_noise, elites)
+    )
     near = [lax.ppermute(block, "cand", [(i, i ^ 2 * k) for i in range(PEERS)]) for k in (1, 2, 3)]
-    own = jnp.stack([block, *near])
-    return own, lax.ppermute(own, "cand", [(i, i ^ 1) for i in range(PEERS)])
-
-
-def body(params, h_start, z_start, action_noise, state_noise, elites):
     a_noise = jnp.pad(
         action_noise.reshape(ITERS, HOR, ACT, COLS), ((0, 0), (0, 0), (0, 8 - ACT), (0, 0))
     ).reshape(ITERS, ROWS, COLS)
@@ -373,7 +386,12 @@
     ids = lax.axis_index("cand") * CANDS_HERE + jnp.arange(CANDS_HERE, dtype=jnp.int32)
     chosen = jnp.any(elites[:, :, :, None] == ids, axis=2).astype(F32)
 
-    weights = prepared(*gathered_params(params))
+    near, a_noise, s_noise, h0, z0, chosen = lax.optimization_barrier(
+        (near, a_noise, s_noise, h0, z0, chosen)
+    )
+    own = jnp.stack([block, *near])
+    other = lax.ppermute(own, "cand", [(i, i ^ 1) for i in range(PEERS)])
+    weights = prepared(own, other)
     rets, bests = [], []
     state = got = None
     for number in range(ITERS):
@@ -397,6 +415,7 @@
         ],
         in_specs=[VMEM] * 7,
         out_specs=[VMEM] * 4,
+        compiler_params=pltpu.CompilerParams(vmem_limit_bytes=4 << 20),
         name="last",
     )(state, got, *rets, *bests)
     return mean.transpose(2, 0, 1), spread.transpose(2, 0, 1), returns, best.T

time: 97.8 us -> 94.2 us (0.963)
  blocking collectives: 44.7 us -> 23.1 us
  starting transfers between devices: 7.49 us -> 19.4 us
  waiting for transfers between devices: 5.5 us -> 12.1 us
  Pallas kernels: 34.3 us -> 32.7 us
  local copies, waits for them, and re-layouts: 4.4 us -> 5.5 us
    all_to_all x1 -> x0, blocking collectives: 20.8 us -> none  [gathered_params(): lax.all_to_all(jnp.broadcast_to(block[None], (32, 8, 256)), 'env', 0, 0,...]
    all_to_all x0 -> x1, starting transfers between devices: none -> 11.9 us  [from_env(): lax.all_to_all(jnp.broadcast_to(block[None], (32, 8, 256)), 'env', 0, 0,...]
    all_to_all x0 -> x1, waiting for transfers between devices: none -> 8.98 us  [from_env(): lax.all_to_all(jnp.broadcast_to(block[None], (32, 8, 256)), 'env', 0, 0,...]
    ppermute x4, waiting for transfers between devices: 5.5 us -> 3.15 us  [the longest x3 1.62 us: body(): lax.ppermute(block, 'cand', [(i, i ^ 2 * k) for i in range(PEERS)])]
    reshape x1, local copies, waits for them, and re-layouts: 0.35 us -> 2.05 us  [body(): state_noise.reshape(ITERS, HOR, STOCH, COLS)]
    unnamed x26 -> x12, local copies, waits for them, and re-layouts: 3.37 us -> 2.13 us
  transfers between devices with their start and end apart: 4 -> 5, of which waited for: 2 -> 4; matrix products, arithmetic and copies ran while one was open for 1% -> 3% of each run, Pallas kernels for 0% -> 0%
where the time goes in v3:
time: 94.2 us; the launch traced here: 93.8 us
  Pallas kernels  32.7 us (35%)
  blocking collectives  23.1 us (25%)
  starting transfers between devices  19.4 us (21%)
  waiting for transfers between devices  12.1 us (13%)
  local copies, waits for them, and re-layouts  5.5 us (6%)
    pallas_call x3, Pallas kernels, rollout(): pl.pallas_call(functools.partial(rollout_kernel, first, number), out_shap...  31.1 us
    all_to_all x3, blocking collectives, body(): got = lax.all_to_all(out[1], 'cand', 0, 0, tiled=True)  23.1 us
    all_to_all x1, starting transfers between devices, from_env(): lax.all_to_all(jnp.broadcast_to(block[None], (32, 8, 256)), 'env', 0, 0,...  11.9 us
    all_to_all x1, waiting for transfers between devices, from_env(): lax.all_to_all(jnp.broadcast_to(block[None], (32, 8, 256)), 'env', 0, 0,...  8.98 us
    ppermute x3, starting transfers between devices, body(): lax.ppermute(block, 'cand', [(i, i ^ 2 * k) for i in range(PEERS)])  3.92 us
    ppermute x1, starting transfers between devices, body(): other = lax.ppermute(own, 'cand', [(i, i ^ 1) for i in range(PEERS)])  3.57 us
    unnamed x12, local copies, waits for them, and re-layouts  2.13 us
    reshape x1, local copies, waits for them, and re-layouts, body(): state_noise.reshape(ITERS, HOR, STOCH, COLS)  2.05 us
  transfers between devices with their start and end apart: 5, of which 4 were waited for; matrix products, arithmetic and copies ran while one was open for 3% of the time, Pallas kernels for 0%

profile of v3, /device:TPU:1, one launch (start us, length us, event | category | flops | bytes accessed | tf_op | source)
XLA Modules:
  0.0 93.8 jit_solution(3331895713289326103)
XLA Ops:
  0.7 0.0 copy-start.1
  0.7 0.7 copy-done.1
  1.3 0.2 dynamic_update_slice.3
  1.5 0.1 reshape.27
  1.6 0.7 broadcast_in_dim.9
  2.3 11.9 %all-to-all-start = ((bf16[32,8,256]{2,1,0:T(8,128)(2,1)}), bf16[32,8,256]{2,1,0:T(8,128)(2,1)S(1)}, u32[]{:S(2)}, u32[]{:S(2)}) async-start(bf16[32,8,256]{2,1,0:T(8,128)(2,1)} %broadcast_in_dim.9), calls=%async_computation | async-start | bytes 262144 | tf_op jit(solution)/shard_map/all_to_all | solution.py:366
  14.2 0.1 pad.25.clone
  14.2 0.0 copy-start.3
  14.2 0.1 pad.26.clone
  14.3 0.0 copy-start.2
  14.3 9.0 %all-to-all-done = bf16[32,8,256]{2,1,0:T(8,128)(2,1)S(1)} async-done(((bf16[32,8,256]{2,1,0:T(8,128)(2,1)}), bf16[32,8,256]{2,1,0:T(8,128)(2,1)S(1)}, u32[]{:S(2)}, u32[]{:S(2)}) %all-to-all-start) | async-done | bytes 131104 | tf_op jit(solution)/shard_map/all_to_all | solution.py:366
  23.3 1.3 %collective-permute-start = (bf16[32,8,256]{2,1,0:T(8,128)(2,1)S(1)}, bf16[32,8,256]{2,1,0:T(8,128)(2,1)S(1)}, u32[]{:S(2)}, u32[]{:S(2)}) collective-permute-start(bf16[32,8,256]{2,1,0:T(8,128)(2,1)S(1)} %all-to-all-done), channel_id=1, source_target_pairs={{0,2},{1,3},{2,0},{3,1},{4,6},{5,7},{6,4},{7,5},{8,10},{9,11},{10,... | collective-permute-start | bytes 393224 | tf_op jit(solution)/shard_map/ppermute | solution.py:374
  24.6 2.6 %collective-permute-start.1 = (bf16[32,8,256]{2,1,0:T(8,128)(2,1)S(1)}, bf16[32,8,256]{2,1,0:T(8,128)(2,1)S(1)}, u32[]{:S(2)}, u32[]{:S(2)}) collective-permute-start(bf16[32,8,256]{2,1,0:T(8,128)(2,1)S(1)} %all-to-all-done), channel_id=1, source_target_pairs={{0,4},{1,5},{2,6},{3,7},{4,0},{5,1},{6,2},{7,3},{8,12},{9,13},{10,... | collective-permute-start | bytes 393224 | tf_op jit(solution)/shard_map/ppermute | solution.py:374
  27.2 0.0 collective-permute-start.2
  27.2 0.0 copy-done.3
  27.2 0.0 copy-done.2
  27.2 0.2 compare_reduce_fusion
  27.4 2.0 %reshape.30 = bf16[3,12,30,256]{3,2,1,0:T(8,128)(2,1)S(1)} reshape(bf16[3,12,30,2,128]{4,3,2,1,0:T(2,128)(2,1)} %param.11) | data formatting | bytes 1105920 | tf_op jit(solution)/shard_map/reshape | solution.py:379
  29.5 0.0 copy-start
  29.5 0.1 pad.18.s_noise
  29.6 0.8 copy-done
  30.4 0.0 copy-start.4
  30.4 0.1 reshape.28
  30.5 0.6 copy-done.4
  31.1 0.0 collective-permute-done
  31.1 0.1 collective-permute-done.1
  31.2 1.5 %collective-permute-done.2 = bf16[32,8,256]{2,1,0:T(8,128)(2,1)S(1)} collective-permute-done((bf16[32,8,256]{2,1,0:T(8,128)(2,1)S(1)}, bf16[32,8,256]{2,1,0:T(8,128)(2,1)S(1)}, u32[]{:S(2)}, u32[]{:S(2)}) %collective-permute-start.2) | collective-permute-done | bytes 131104 | tf_op jit(solution)/shard_map/ppermute | solution.py:374
  32.7 0.1 pad_maximum_fusion.own
  32.8 3.6 %collective-permute-start.3 = (bf16[4,32,8,256]{3,2,1,0:T(8,128)(2,1)S(1)}, bf16[4,32,8,256]{3,2,1,0:T(8,128)(2,1)S(1)}, u32[]{:S(2)}, u32[]{:S(2)}) collective-permute-start(bf16[4,32,8,256]{3,2,1,0:T(8,128)(2,1)S(1)} %pad_maximum_fusion.own), channel_id=1, source_target_pairs={{0,1},{1,0},{2,3},{3,2},{4,5},{5,4},{6,7},{7,6},{8,9},{9,8},{10,11... | collective-permute-start | bytes 1572872 | tf_op jit(solution)/shard_map/ppermute | solution.py:393
  36.4 1.5 %collective-permute-done.3.other = bf16[4,32,8,256]{3,2,1,0:T(8,128)(2,1)S(1)} collective-permute-done((bf16[4,32,8,256]{3,2,1,0:T(8,128)(2,1)S(1)}, bf16[4,32,8,256]{3,2,1,0:T(8,128)(2,1)S(1)}, u32[]{:S(2)}, u32[]{:S(2)}) %collective-permute-start.3) | collective-permute-done | bytes 524320 | tf_op jit(solution)/shard_map/ppermute | solution.py:393
  37.9 0.6 prepare.1
  38.5 10.0 %rollout_0.1 = (f32[2,128]{1,0:T(2,128)S(1)}, f32[8,8,128]{2,1,0:T(8,128)S(1)}) custom-call(bf16[256,1024]{1,0:T(8,128)(2,1)S(1)} %get-tuple-element.48.w_h, bf16[256,768]{1,0:T(8,128)(2,1)S(1)} %get-tuple-element.49.w_x, bf16[128,256]{1,0:T(8,128)(2,1)S(1)} %get-tuple-element.50.w_1, bf16[256,256]{1,0:T(8,128)(2,1)S(1)} %get-tuple-element.51.w_5, ...), custom_call_target="tpu_custom_call" | custom-call | tf_op jit(solution)/shard_map/rollout_0/pallas_call | solution.py:225
  48.5 0.0 copy-start.5
  48.6 7.4 %all_to_all.20.rest_1_ = f32[8,8,128]{2,1,0:T(8,128)S(1)} all-to-all(f32[8,8,128]{2,1,0:T(8,128)S(1)} %get-tuple-element.60), channel_id=1, replica_groups=mesh['env'=32,'cand'=8] {'cand'}, dimensions={0} | all-to-all | bytes 65536 | tf_op jit(solution)/shard_map/all_to_all | solution.py:407
  56.0 0.0 copy-done.5
  56.0 0.1 broadcast_in_dim.11.rest_0_
  56.1 10.5 %rollout_1.1 = (f32[2,128]{1,0:T(2,128)S(1)}, f32[8,8,128]{2,1,0:T(8,128)S(1)}, f32[8,128]{1,0:T(8,128)S(1)}, f32[2,128]{1,0:T(2,128)S(1)}) custom-call(bf16[256,1024]{1,0:T(8,128)(2,1)S(1)} %get-tuple-element.48.w_h, bf16[256,768]{1,0:T(8,128)(2,1)S(1)} %get-tuple-element.49.w_x, bf16[128,256]{1,0:T(8,128)(2,1)S(1)} %get-tuple-element.50.w_1, ...), custom_call_target="tpu_custom_call" | custom-call | tf_op jit(solution)/shard_map/rollout_1/pallas_call | solution.py:225
  66.6 7.8 %all_to_all.21.rest_1_ = f32[8,8,128]{2,1,0:T(8,128)S(1)} all-to-all(f32[8,8,128]{2,1,0:T(8,128)S(1)} %get-tuple-element.62), channel_id=1, replica_groups=mesh['env'=32,'cand'=8] {'cand'}, dimensions={0} | all-to-all | bytes 65536 | tf_op jit(solution)/shard_map/all_to_all | solution.py:407
  74.4 10.5 %rollout_2.1 = (f32[2,128]{1,0:T(2,128)S(1)}, f32[8,8,128]{2,1,0:T(8,128)S(1)}, f32[8,128]{1,0:T(8,128)S(1)}, f32[2,128]{1,0:T(2,128)S(1)}) custom-call(bf16[256,1024]{1,0:T(8,128)(2,1)S(1)} %get-tuple-element.48.w_h, bf16[256,768]{1,0:T(8,128)(2,1)S(1)} %get-tuple-element.49.w_x, bf16[128,256]{1,0:T(8,128)(2,1)S(1)} %get-tuple-element.50.w_1, ...), custom_call_target="tpu_custom_call" | custom-call | tf_op jit(solution)/shard_map/rollout_2/pallas_call | solution.py:225
  85.0 7.8 %all_to_all.22.got_ref = f32[8,8,128]{2,1,0:T(8,128)S(1)} all-to-all(f32[8,8,128]{2,1,0:T(8,128)S(1)} %get-tuple-element.64), channel_id=1, replica_groups=mesh['env'=32,'cand'=8] {'cand'}, dimensions={0} | all-to-all | bytes 65536 | tf_op jit(solution)/shard_map/all_to_all | solution.py:407
  92.8 1.0 %last.1 = (f32[6,2,12]{2,1,0:T(2,128)}, f32[6,2,12]{2,1,0:T(2,128)}, f32[3,2,128]{2,1,0:T(2,128)}, f32[2,3]{1,0:T(2,128)}) custom-call(f32[8,128]{1,0:T(8,128)S(1)} %get-tuple-element.63.state_ref, f32[8,8,128]{2,1,0:T(8,128)S(1)} %all_to_all.22.got_ref, f32[2,128]{1,0:T(2,128)S(1)} %get-tuple-element.65.r0, f32[2,128]{1,0:T(2,128)S(1)} %get-tuple-element.66.r1, ...), custom_call_target="tpu_custom_call" | custom-call | tf_op jit(solution)/shard_map/last/pallas_call | solution.py:408
  (9 shorter events, 0.1 us)
Async XLA Ops:
  0.7 0.7 copy-start.1
  2.3 21.0 %all-to-all-start = ((bf16[32,8,256]{2,1,0:T(8,128)(2,1)}), bf16[32,8,256]{2,1,0:T(8,128)(2,1)S(1)}, u32[]{:S(2)}, u32[]{:S(2)}) async-start(bf16[32,8,256]{2,1,0:T(8,128)(2,1)} %broadcast_in_dim.9), calls=%async_computation | async-start | bytes 262144 | tf_op jit(solution)/shard_map/all_to_all | solution.py:366
  14.2 13.0 %copy-start.3 = (f32[2,200]{1,0:T(2,128)S(1)}, f32[2,200]{1,0:T(2,128)}, u32[]{:S(2)}) copy-start(f32[2,200]{1,0:T(2,128)} %param.8) | copy-start | bytes 4804
  14.3 12.9 %copy-start.2 = (s32[3,2,100]{2,1,0:T(2,128)S(1)}, s32[3,2,100]{2,1,0:T(2,128)}, u32[]{:S(2)}) copy-start(s32[3,2,100]{2,1,0:T(2,128)} %param.12) | copy-start | bytes 7204
  23.3 7.8 %collective-permute-start = (bf16[32,8,256]{2,1,0:T(8,128)(2,1)S(1)}, bf16[32,8,256]{2,1,0:T(8,128)(2,1)S(1)}, u32[]{:S(2)}, u32[]{:S(2)}) collective-permute-start(bf16[32,8,256]{2,1,0:T(8,128)(2,1)S(1)} %all-to-all-done), channel_id=1, source_target_pairs={{0,2},{1,3},{2,0},{3,1},{4,6},{5,7},{6,4},{7,5},{8,10},{9,11},{10,... | collective-permute-start | bytes 393224 | tf_op jit(solution)/shard_map/ppermute | solution.py:374
  24.6 6.6 %collective-permute-start.1 = (bf16[32,8,256]{2,1,0:T(8,128)(2,1)S(1)}, bf16[32,8,256]{2,1,0:T(8,128)(2,1)S(1)}, u32[]{:S(2)}, u32[]{:S(2)}) collective-permute-start(bf16[32,8,256]{2,1,0:T(8,128)(2,1)S(1)} %all-to-all-done), channel_id=1, source_target_pairs={{0,4},{1,5},{2,6},{3,7},{4,0},{5,1},{6,2},{7,3},{8,12},{9,13},{10,... | collective-permute-start | bytes 393224 | tf_op jit(solution)/shard_map/ppermute | solution.py:374
  27.2 5.5 %collective-permute-start.2 = (bf16[32,8,256]{2,1,0:T(8,128)(2,1)S(1)}, bf16[32,8,256]{2,1,0:T(8,128)(2,1)S(1)}, u32[]{:S(2)}, u32[]{:S(2)}) collective-permute-start(bf16[32,8,256]{2,1,0:T(8,128)(2,1)S(1)} %all-to-all-done), channel_id=1, source_target_pairs={{0,6},{1,7},{2,4},{3,5},{4,2},{5,3},{6,0},{7,1},{8,14},{9,15},{10,... | collective-permute-start | bytes 393224 | tf_op jit(solution)/shard_map/ppermute | solution.py:374
  29.5 0.9 copy-start
  30.4 0.7 copy-start.4
  32.8 5.1 %collective-permute-start.3 = (bf16[4,32,8,256]{3,2,1,0:T(8,128)(2,1)S(1)}, bf16[4,32,8,256]{3,2,1,0:T(8,128)(2,1)S(1)}, u32[]{:S(2)}, u32[]{:S(2)}) collective-permute-start(bf16[4,32,8,256]{3,2,1,0:T(8,128)(2,1)S(1)} %pad_maximum_fusion.own), channel_id=1, source_target_pairs={{0,1},{1,0},{2,3},{3,2},{4,5},{5,4},{6,7},{7,6},{8,9},{9,8},{10,11... | collective-permute-start | bytes 1572872 | tf_op jit(solution)/shard_map/ppermute | solution.py:393
  48.5 7.5 %copy-start.5 = (f32[8]{0:T(128)S(1)}, f32[8]{0:T(128)}, u32[]{:S(2)}) copy-start(f32[8]{0:T(128)} %constant.40.clone) | copy-start | bytes 100

commit v4 on v3

--- a/solution.py
+++ b/solution.py
@@ -125,18 +125,22 @@
             scale = jnp.where(in_latent, softplus(s[:, 128:]) + min_scale, 1.0)
             n = s_noise[number, t - 1].astype(F32)
             za = (s[:, :128] + scale * drawn(min(t, HOR - 1), n)).astype(BF16)
-            q = scaled_elu(dot(hd, w_h[:, 768:]) + dot(za, w_6z[...]), S230)
+        if t == HOR:
+            q = scaled_elu(dot(hd, w_h[:, 768:]) + dot(za[:, :48], w_6z[:48]), S230)
             q = q.astype(BF16).astype(F32)
             q_sum = q if q_sum is None else q_sum + q
-        if t == HOR:
             break
-        x = scaled_elu(dot(za, w_1[...]), S36).astype(BF16)
+        x = scaled_elu(dot(za[:, :48], w_1[:48]), S36).astype(BF16)
         gates = dot(x, w_x[:, :512]) + dot(hd, w_h[:, :512])
         half = 0.5 * h
         rh = (half + jnp.tanh(gates[:, :256] * (0.5 * S400)) * half).astype(BF16)
         update = 0.5 + 0.5 * jnp.tanh(gates[:, 256:] * (0.5 * S400))
         proposal = jnp.tanh((dot(x, w_x[:, 512:]) + dot(rh, w_r[...])) * S400)
         h = proposal + update * (h - proposal)
+        if t > 0:
+            q = scaled_elu(dot(hd, w_h[:, 768:]) + dot(za[:, :48], w_6z[:48]), S230)
+            q = q.astype(BF16).astype(F32)
+            q_sum = q if q_sum is None else q_sum + q
 
     wide = lax.broadcasted_iota(jnp.int32, (1, COLS), 1)
     wide16 = lax.broadcasted_iota(jnp.int32, (16, COLS), 1) // CANDS_HERE

time: 94.2 us -> 93.3 us (level)
  no operation moved by 1% of the time
where the time goes in v4:
time: 93.3 us; the launch traced here: 92.9 us
  Pallas kernels  31.8 us (34%)
  blocking collectives  23.1 us (25%)
  starting transfers between devices  19.4 us (21%)
  waiting for transfers between devices  12.1 us (13%)
  local copies, waits for them, and re-layouts  5.5 us (6%)
    pallas_call x3, Pallas kernels, rollout(): pl.pallas_call(functools.partial(rollout_kernel, first, number), out_shap...  30.2 us
    all_to_all x3, blocking collectives, body(): got = lax.all_to_all(out[1], 'cand', 0, 0, tiled=True)  23.1 us
    all_to_all x1, starting transfers between devices, from_env(): lax.all_to_all(jnp.broadcast_to(block[None], (32, 8, 256)), 'env', 0, 0,...  11.9 us
    all_to_all x1, waiting for transfers between devices, from_env(): lax.all_to_all(jnp.broadcast_to(block[None], (32, 8, 256)), 'env', 0, 0,...  8.98 us
    ppermute x3, starting transfers between devices, body(): lax.ppermute(block, 'cand', [(i, i ^ 2 * k) for i in range(PEERS)])  3.92 us
    ppermute x1, starting transfers between devices, body(): other = lax.ppermute(own, 'cand', [(i, i ^ 1) for i in range(PEERS)])  3.57 us
    unnamed x12, local copies, waits for them, and re-layouts  2.13 us
    reshape x1, local copies, waits for them, and re-layouts, body(): state_noise.reshape(ITERS, HOR, STOCH, COLS)  2.05 us
  transfers between devices with their start and end apart: 5, of which 4 were waited for; matrix products, arithmetic and copies ran while one was open for 3% of the time, Pallas kernels for 0%

profile of v4, /device:TPU:1, one launch (start us, length us, event | category | flops | bytes accessed | tf_op | source)
XLA Modules:
  0.0 92.9 jit_solution(3098906344237671137)
XLA Ops:
  0.7 0.0 copy-start.1
  0.7 0.7 copy-done.1
  1.3 0.2 dynamic_update_slice.3
  1.5 0.1 reshape.27
  1.6 0.7 broadcast_in_dim.9
  2.3 11.9 %all-to-all-start = ((bf16[32,8,256]{2,1,0:T(8,128)(2,1)}), bf16[32,8,256]{2,1,0:T(8,128)(2,1)S(1)}, u32[]{:S(2)}, u32[]{:S(2)}) async-start(bf16[32,8,256]{2,1,0:T(8,128)(2,1)} %broadcast_in_dim.9), calls=%async_computation | async-start | bytes 262144 | tf_op jit(solution)/shard_map/all_to_all | solution.py:370
  14.2 0.1 pad.25.clone
  14.2 0.0 copy-start.3
  14.2 0.1 pad.26.clone
  14.3 0.0 copy-start.2
  14.3 9.0 %all-to-all-done = bf16[32,8,256]{2,1,0:T(8,128)(2,1)S(1)} async-done(((bf16[32,8,256]{2,1,0:T(8,128)(2,1)}), bf16[32,8,256]{2,1,0:T(8,128)(2,1)S(1)}, u32[]{:S(2)}, u32[]{:S(2)}) %all-to-all-start) | async-done | bytes 131104 | tf_op jit(solution)/shard_map/all_to_all | solution.py:370
  23.3 1.3 %collective-permute-start = (bf16[32,8,256]{2,1,0:T(8,128)(2,1)S(1)}, bf16[32,8,256]{2,1,0:T(8,128)(2,1)S(1)}, u32[]{:S(2)}, u32[]{:S(2)}) collective-permute-start(bf16[32,8,256]{2,1,0:T(8,128)(2,1)S(1)} %all-to-all-done), channel_id=1, source_target_pairs={{0,2},{1,3},{2,0},{3,1},{4,6},{5,7},{6,4},{7,5},{8,10},{9,11},{10,... | collective-permute-start | bytes 393224 | tf_op jit(solution)/shard_map/ppermute | solution.py:378
  24.6 2.6 %collective-permute-start.1 = (bf16[32,8,256]{2,1,0:T(8,128)(2,1)S(1)}, bf16[32,8,256]{2,1,0:T(8,128)(2,1)S(1)}, u32[]{:S(2)}, u32[]{:S(2)}) collective-permute-start(bf16[32,8,256]{2,1,0:T(8,128)(2,1)S(1)} %all-to-all-done), channel_id=1, source_target_pairs={{0,4},{1,5},{2,6},{3,7},{4,0},{5,1},{6,2},{7,3},{8,12},{9,13},{10,... | collective-permute-start | bytes 393224 | tf_op jit(solution)/shard_map/ppermute | solution.py:378
  27.2 0.0 collective-permute-start.2
  27.2 0.0 copy-done.3
  27.2 0.0 copy-done.2
  27.2 0.2 compare_reduce_fusion
  27.4 2.0 %reshape.30 = bf16[3,12,30,256]{3,2,1,0:T(8,128)(2,1)S(1)} reshape(bf16[3,12,30,2,128]{4,3,2,1,0:T(2,128)(2,1)} %param.11) | data formatting | bytes 1105920 | tf_op jit(solution)/shard_map/reshape | solution.py:383
  29.5 0.0 copy-start
  29.5 0.1 pad.18.s_noise
  29.6 0.8 copy-done
  30.4 0.0 copy-start.4
  30.4 0.1 reshape.28
  30.5 0.6 copy-done.4
  31.1 0.0 collective-permute-done
  31.1 0.1 collective-permute-done.1
  31.2 1.5 %collective-permute-done.2 = bf16[32,8,256]{2,1,0:T(8,128)(2,1)S(1)} collective-permute-done((bf16[32,8,256]{2,1,0:T(8,128)(2,1)S(1)}, bf16[32,8,256]{2,1,0:T(8,128)(2,1)S(1)}, u32[]{:S(2)}, u32[]{:S(2)}) %collective-permute-start.2) | collective-permute-done | bytes 131104 | tf_op jit(solution)/shard_map/ppermute | solution.py:378
  32.7 0.1 pad_maximum_fusion.own
  32.8 3.6 %collective-permute-start.3 = (bf16[4,32,8,256]{3,2,1,0:T(8,128)(2,1)S(1)}, bf16[4,32,8,256]{3,2,1,0:T(8,128)(2,1)S(1)}, u32[]{:S(2)}, u32[]{:S(2)}) collective-permute-start(bf16[4,32,8,256]{3,2,1,0:T(8,128)(2,1)S(1)} %pad_maximum_fusion.own), channel_id=1, source_target_pairs={{0,1},{1,0},{2,3},{3,2},{4,5},{5,4},{6,7},{7,6},{8,9},{9,8},{10,11... | collective-permute-start | bytes 1572872 | tf_op jit(solution)/shard_map/ppermute | solution.py:397
  36.4 1.5 %collective-permute-done.3.other = bf16[4,32,8,256]{3,2,1,0:T(8,128)(2,1)S(1)} collective-permute-done((bf16[4,32,8,256]{3,2,1,0:T(8,128)(2,1)S(1)}, bf16[4,32,8,256]{3,2,1,0:T(8,128)(2,1)S(1)}, u32[]{:S(2)}, u32[]{:S(2)}) %collective-permute-start.3) | collective-permute-done | bytes 524320 | tf_op jit(solution)/shard_map/ppermute | solution.py:397
  37.9 0.6 prepare.1
  38.5 9.7 %rollout_0.1 = (f32[2,128]{1,0:T(2,128)S(1)}, f32[8,8,128]{2,1,0:T(8,128)S(1)}) custom-call(bf16[256,1024]{1,0:T(8,128)(2,1)S(1)} %get-tuple-element.48.w_h, bf16[256,768]{1,0:T(8,128)(2,1)S(1)} %get-tuple-element.49.w_x, bf16[128,256]{1,0:T(8,128)(2,1)S(1)} %get-tuple-element.50.w_1, bf16[256,256]{1,0:T(8,128)(2,1)S(1)} %get-tuple-element.51.w_5, ...), custom_call_target="tpu_custom_call" | custom-call | tf_op jit(solution)/shard_map/rollout_0/pallas_call | solution.py:229
  48.2 0.0 copy-start.5
  48.2 7.5 %all_to_all.20.rest_1_ = f32[8,8,128]{2,1,0:T(8,128)S(1)} all-to-all(f32[8,8,128]{2,1,0:T(8,128)S(1)} %get-tuple-element.60), channel_id=1, replica_groups=mesh['env'=32,'cand'=8] {'cand'}, dimensions={0} | all-to-all | bytes 65536 | tf_op jit(solution)/shard_map/all_to_all | solution.py:411
  55.7 0.0 copy-done.5
  55.7 0.1 broadcast_in_dim.11.rest_0_
  55.8 10.2 %rollout_1.1 = (f32[2,128]{1,0:T(2,128)S(1)}, f32[8,8,128]{2,1,0:T(8,128)S(1)}, f32[8,128]{1,0:T(8,128)S(1)}, f32[2,128]{1,0:T(2,128)S(1)}) custom-call(bf16[256,1024]{1,0:T(8,128)(2,1)S(1)} %get-tuple-element.48.w_h, bf16[256,768]{1,0:T(8,128)(2,1)S(1)} %get-tuple-element.49.w_x, bf16[128,256]{1,0:T(8,128)(2,1)S(1)} %get-tuple-element.50.w_1, ...), custom_call_target="tpu_custom_call" | custom-call | tf_op jit(solution)/shard_map/rollout_1/pallas_call | solution.py:229
  66.0 7.8 %all_to_all.21.rest_1_ = f32[8,8,128]{2,1,0:T(8,128)S(1)} all-to-all(f32[8,8,128]{2,1,0:T(8,128)S(1)} %get-tuple-element.62), channel_id=1, replica_groups=mesh['env'=32,'cand'=8] {'cand'}, dimensions={0} | all-to-all | bytes 65536 | tf_op jit(solution)/shard_map/all_to_all | solution.py:411
  73.9 10.2 %rollout_2.1 = (f32[2,128]{1,0:T(2,128)S(1)}, f32[8,8,128]{2,1,0:T(8,128)S(1)}, f32[8,128]{1,0:T(8,128)S(1)}, f32[2,128]{1,0:T(2,128)S(1)}) custom-call(bf16[256,1024]{1,0:T(8,128)(2,1)S(1)} %get-tuple-element.48.w_h, bf16[256,768]{1,0:T(8,128)(2,1)S(1)} %get-tuple-element.49.w_x, bf16[128,256]{1,0:T(8,128)(2,1)S(1)} %get-tuple-element.50.w_1, ...), custom_call_target="tpu_custom_call" | custom-call | tf_op jit(solution)/shard_map/rollout_2/pallas_call | solution.py:229
  84.1 7.8 %all_to_all.22.got_ref = f32[8,8,128]{2,1,0:T(8,128)S(1)} all-to-all(f32[8,8,128]{2,1,0:T(8,128)S(1)} %get-tuple-element.64), channel_id=1, replica_groups=mesh['env'=32,'cand'=8] {'cand'}, dimensions={0} | all-to-all | bytes 65536 | tf_op jit(solution)/shard_map/all_to_all | solution.py:411
  91.9 1.0 %last.1 = (f32[6,2,12]{2,1,0:T(2,128)}, f32[6,2,12]{2,1,0:T(2,128)}, f32[3,2,128]{2,1,0:T(2,128)}, f32[2,3]{1,0:T(2,128)}) custom-call(f32[8,128]{1,0:T(8,128)S(1)} %get-tuple-element.63.state_ref, f32[8,8,128]{2,1,0:T(8,128)S(1)} %all_to_all.22.got_ref, f32[2,128]{1,0:T(2,128)S(1)} %get-tuple-element.65.r0, f32[2,128]{1,0:T(2,128)S(1)} %get-tuple-element.66.r1, ...), custom_call_target="tpu_custom_call" | custom-call | tf_op jit(solution)/shard_map/last/pallas_call | solution.py:412
  (9 shorter events, 0.1 us)
Async XLA Ops:
  0.7 0.7 copy-start.1
  2.3 21.0 %all-to-all-start = ((bf16[32,8,256]{2,1,0:T(8,128)(2,1)}), bf16[32,8,256]{2,1,0:T(8,128)(2,1)S(1)}, u32[]{:S(2)}, u32[]{:S(2)}) async-start(bf16[32,8,256]{2,1,0:T(8,128)(2,1)} %broadcast_in_dim.9), calls=%async_computation | async-start | bytes 262144 | tf_op jit(solution)/shard_map/all_to_all | solution.py:370
  14.2 13.0 %copy-start.3 = (f32[2,200]{1,0:T(2,128)S(1)}, f32[2,200]{1,0:T(2,128)}, u32[]{:S(2)}) copy-start(f32[2,200]{1,0:T(2,128)} %param.8) | copy-start | bytes 4804
  14.3 12.9 %copy-start.2 = (s32[3,2,100]{2,1,0:T(2,128)S(1)}, s32[3,2,100]{2,1,0:T(2,128)}, u32[]{:S(2)}) copy-start(s32[3,2,100]{2,1,0:T(2,128)} %param.12) | copy-start | bytes 7204
  23.3 7.8 %collective-permute-start = (bf16[32,8,256]{2,1,0:T(8,128)(2,1)S(1)}, bf16[32,8,256]{2,1,0:T(8,128)(2,1)S(1)}, u32[]{:S(2)}, u32[]{:S(2)}) collective-permute-start(bf16[32,8,256]{2,1,0:T(8,128)(2,1)S(1)} %all-to-all-done), channel_id=1, source_target_pairs={{0,2},{1,3},{2,0},{3,1},{4,6},{5,7},{6,4},{7,5},{8,10},{9,11},{10,... | collective-permute-start | bytes 393224 | tf_op jit(solution)/shard_map/ppermute | solution.py:378
  24.6 6.6 %collective-permute-start.1 = (bf16[32,8,256]{2,1,0:T(8,128)(2,1)S(1)}, bf16[32,8,256]{2,1,0:T(8,128)(2,1)S(1)}, u32[]{:S(2)}, u32[]{:S(2)}) collective-permute-start(bf16[32,8,256]{2,1,0:T(8,128)(2,1)S(1)} %all-to-all-done), channel_id=1, source_target_pairs={{0,4},{1,5},{2,6},{3,7},{4,0},{5,1},{6,2},{7,3},{8,12},{9,13},{10,... | collective-permute-start | bytes 393224 | tf_op jit(solution)/shard_map/ppermute | solution.py:378
  27.2 5.5 %collective-permute-start.2 = (bf16[32,8,256]{2,1,0:T(8,128)(2,1)S(1)}, bf16[32,8,256]{2,1,0:T(8,128)(2,1)S(1)}, u32[]{:S(2)}, u32[]{:S(2)}) collective-permute-start(bf16[32,8,256]{2,1,0:T(8,128)(2,1)S(1)} %all-to-all-done), channel_id=1, source_target_pairs={{0,6},{1,7},{2,4},{3,5},{4,2},{5,3},{6,0},{7,1},{8,14},{9,15},{10,... | collective-permute-start | bytes 393224 | tf_op jit(solution)/shard_map/ppermute | solution.py:378
  29.5 0.9 copy-start
  30.4 0.7 copy-start.4
  32.8 5.1 %collective-permute-start.3 = (bf16[4,32,8,256]{3,2,1,0:T(8,128)(2,1)S(1)}, bf16[4,32,8,256]{3,2,1,0:T(8,128)(2,1)S(1)}, u32[]{:S(2)}, u32[]{:S(2)}) collective-permute-start(bf16[4,32,8,256]{3,2,1,0:T(8,128)(2,1)S(1)} %pad_maximum_fusion.own), channel_id=1, source_target_pairs={{0,1},{1,0},{2,3},{3,2},{4,5},{5,4},{6,7},{7,6},{8,9},{9,8},{10,11... | collective-permute-start | bytes 1572872 | tf_op jit(solution)/shard_map/ppermute | solution.py:397
  48.2 7.5 %copy-start.5 = (f32[8]{0:T(128)S(1)}, f32[8]{0:T(128)}, u32[]{:S(2)}) copy-start(f32[8]{0:T(128)} %constant.40.clone) | copy-start | bytes 100

commit v5 on v4

--- a/solution.py
+++ b/solution.py
@@ -239,7 +239,7 @@
 
 PART = 1355
 ROW = 200
-TABLE = 1736
+TABLE = 1752
 
 
 def prepare_kernel(own, other, w_h, w_x, w_1, w_5, w_6z, w_r, w_7, blocks, left, right, fifth_l, fifth_r):
@@ -321,7 +321,7 @@
     last_row = rows(1501, 8)
     mean, scale = halves(last_row)
     bias = jnp.concatenate([mean, scale], 1)[0:1]
-    w_5[...] = filled([jnp.concatenate([fifth_l[...], fifth_r[...]], 1), foot(bias, 200)])
+    w_5[...] = filled([jnp.concatenate([fifth_l[:200], fifth_r[:200]], 1), foot(bias, 200)])
 
     def shifted(start, count):
         one = pltpu.roll(rows(start, count), 256 - 60, 1)
@@ -355,8 +355,8 @@
             pltpu.VMEM((PEERS, 32, 8, 256), BF16),
             pltpu.VMEM((TABLE, 128), F32),
             pltpu.VMEM((TABLE, 128), F32),
-            pltpu.VMEM((200, 128), F32),
-            pltpu.VMEM((200, 128), F32),
+            pltpu.VMEM((256, 128), F32),
+            pltpu.VMEM((256, 128), F32),
         ],
         compiler_params=pltpu.CompilerParams(vmem_limit_bytes=40 << 20),
         name="prepare",

time: 93.3 us -> 93.3 us (level)
  no operation moved by 1% of the time
where the time goes in v5:
time: 93.3 us; the launch traced here: 92.9 us
  Pallas kernels  31.8 us (34%)
  blocking collectives  23.1 us (25%)
  starting transfers between devices  19.4 us (21%)
  waiting for transfers between devices  12.1 us (13%)
  local copies, waits for them, and re-layouts  5.5 us (6%)
    pallas_call x3, Pallas kernels, rollout(): pl.pallas_call(functools.partial(rollout_kernel, first, number), out_shap...  30.2 us
    all_to_all x3, blocking collectives, body(): got = lax.all_to_all(out[1], 'cand', 0, 0, tiled=True)  23.1 us
    all_to_all x1, starting transfers between devices, from_env(): lax.all_to_all(jnp.broadcast_to(block[None], (32, 8, 256)), 'env', 0, 0,...  11.9 us
    all_to_all x1, waiting for transfers between devices, from_env(): lax.all_to_all(jnp.broadcast_to(block[None], (32, 8, 256)), 'env', 0, 0,...  8.98 us
    ppermute x3, starting transfers between devices, body(): lax.ppermute(block, 'cand', [(i, i ^ 2 * k) for i in range(PEERS)])  3.92 us
    ppermute x1, starting transfers between devices, body(): other = lax.ppermute(own, 'cand', [(i, i ^ 1) for i in range(PEERS)])  3.57 us
    unnamed x12, local copies, waits for them, and re-layouts  2.13 us
    reshape x1, local copies, waits for them, and re-layouts, body(): state_noise.reshape(ITERS, HOR, STOCH, COLS)  2.05 us
  transfers between devices with their start and end apart: 5, of which 4 were waited for; matrix products, arithmetic and copies ran while one was open for 3% of the time, Pallas kernels for 0%

profile of v5, /device:TPU:1, one launch (start us, length us, event | category | flops | bytes accessed | tf_op | source)
XLA Modules:
  0.0 92.9 jit_solution(8776840496292366976)
XLA Ops:
  0.7 0.0 copy-start.1
  0.7 0.7 copy-done.1
  1.3 0.2 dynamic_update_slice.3
  1.5 0.1 reshape.27
  1.6 0.7 broadcast_in_dim.9
  2.3 11.9 %all-to-all-start = ((bf16[32,8,256]{2,1,0:T(8,128)(2,1)}), bf16[32,8,256]{2,1,0:T(8,128)(2,1)S(1)}, u32[]{:S(2)}, u32[]{:S(2)}) async-start(bf16[32,8,256]{2,1,0:T(8,128)(2,1)} %broadcast_in_dim.9), calls=%async_computation | async-start | bytes 262144 | tf_op jit(solution)/shard_map/all_to_all | solution.py:370
  14.2 0.1 pad.25.clone
  14.2 0.0 copy-start.3
  14.2 0.1 pad.26.clone
  14.3 0.0 copy-start.2
  14.3 9.0 %all-to-all-done = bf16[32,8,256]{2,1,0:T(8,128)(2,1)S(1)} async-done(((bf16[32,8,256]{2,1,0:T(8,128)(2,1)}), bf16[32,8,256]{2,1,0:T(8,128)(2,1)S(1)}, u32[]{:S(2)}, u32[]{:S(2)}) %all-to-all-start) | async-done | bytes 131104 | tf_op jit(solution)/shard_map/all_to_all | solution.py:370
  23.3 1.3 %collective-permute-start = (bf16[32,8,256]{2,1,0:T(8,128)(2,1)S(1)}, bf16[32,8,256]{2,1,0:T(8,128)(2,1)S(1)}, u32[]{:S(2)}, u32[]{:S(2)}) collective-permute-start(bf16[32,8,256]{2,1,0:T(8,128)(2,1)S(1)} %all-to-all-done), channel_id=1, source_target_pairs={{0,2},{1,3},{2,0},{3,1},{4,6},{5,7},{6,4},{7,5},{8,10},{9,11},{10,... | collective-permute-start | bytes 393224 | tf_op jit(solution)/shard_map/ppermute | solution.py:378
  24.6 2.6 %collective-permute-start.1 = (bf16[32,8,256]{2,1,0:T(8,128)(2,1)S(1)}, bf16[32,8,256]{2,1,0:T(8,128)(2,1)S(1)}, u32[]{:S(2)}, u32[]{:S(2)}) collective-permute-start(bf16[32,8,256]{2,1,0:T(8,128)(2,1)S(1)} %all-to-all-done), channel_id=1, source_target_pairs={{0,4},{1,5},{2,6},{3,7},{4,0},{5,1},{6,2},{7,3},{8,12},{9,13},{10,... | collective-permute-start | bytes 393224 | tf_op jit(solution)/shard_map/ppermute | solution.py:378
  27.2 0.0 collective-permute-start.2
  27.2 0.0 copy-done.3
  27.2 0.0 copy-done.2
  27.2 0.2 compare_reduce_fusion
  27.4 2.0 %reshape.30 = bf16[3,12,30,256]{3,2,1,0:T(8,128)(2,1)S(1)} reshape(bf16[3,12,30,2,128]{4,3,2,1,0:T(2,128)(2,1)} %param.11) | data formatting | bytes 1105920 | tf_op jit(solution)/shard_map/reshape | solution.py:383
  29.5 0.0 copy-start
  29.5 0.1 pad.18.s_noise
  29.6 0.8 copy-done
  30.4 0.0 copy-start.4
  30.4 0.1 reshape.28
  30.5 0.6 copy-done.4
  31.1 0.0 collective-permute-done
  31.1 0.1 collective-permute-done.1
  31.2 1.5 %collective-permute-done.2 = bf16[32,8,256]{2,1,0:T(8,128)(2,1)S(1)} collective-permute-done((bf16[32,8,256]{2,1,0:T(8,128)(2,1)S(1)}, bf16[32,8,256]{2,1,0:T(8,128)(2,1)S(1)}, u32[]{:S(2)}, u32[]{:S(2)}) %collective-permute-start.2) | collective-permute-done | bytes 131104 | tf_op jit(solution)/shard_map/ppermute | solution.py:378
  32.7 0.1 pad_maximum_fusion.own
  32.8 3.6 %collective-permute-start.3 = (bf16[4,32,8,256]{3,2,1,0:T(8,128)(2,1)S(1)}, bf16[4,32,8,256]{3,2,1,0:T(8,128)(2,1)S(1)}, u32[]{:S(2)}, u32[]{:S(2)}) collective-permute-start(bf16[4,32,8,256]{3,2,1,0:T(8,128)(2,1)S(1)} %pad_maximum_fusion.own), channel_id=1, source_target_pairs={{0,1},{1,0},{2,3},{3,2},{4,5},{5,4},{6,7},{7,6},{8,9},{9,8},{10,11... | collective-permute-start | bytes 1572872 | tf_op jit(solution)/shard_map/ppermute | solution.py:397
  36.4 1.5 %collective-permute-done.3.other = bf16[4,32,8,256]{3,2,1,0:T(8,128)(2,1)S(1)} collective-permute-done((bf16[4,32,8,256]{3,2,1,0:T(8,128)(2,1)S(1)}, bf16[4,32,8,256]{3,2,1,0:T(8,128)(2,1)S(1)}, u32[]{:S(2)}, u32[]{:S(2)}) %collective-permute-start.3) | collective-permute-done | bytes 524320 | tf_op jit(solution)/shard_map/ppermute | solution.py:397
  37.9 0.6 prepare.1
  38.5 9.7 %rollout_0.1 = (f32[2,128]{1,0:T(2,128)S(1)}, f32[8,8,128]{2,1,0:T(8,128)S(1)}) custom-call(bf16[256,1024]{1,0:T(8,128)(2,1)S(1)} %get-tuple-element.48.w_h, bf16[256,768]{1,0:T(8,128)(2,1)S(1)} %get-tuple-element.49.w_x, bf16[128,256]{1,0:T(8,128)(2,1)S(1)} %get-tuple-element.50.w_1, bf16[256,256]{1,0:T(8,128)(2,1)S(1)} %get-tuple-element.51.w_5, ...), custom_call_target="tpu_custom_call" | custom-call | tf_op jit(solution)/shard_map/rollout_0/pallas_call | solution.py:229
  48.2 0.0 copy-start.5
  48.2 7.5 %all_to_all.20.rest_1_ = f32[8,8,128]{2,1,0:T(8,128)S(1)} all-to-all(f32[8,8,128]{2,1,0:T(8,128)S(1)} %get-tuple-element.60), channel_id=1, replica_groups=mesh['env'=32,'cand'=8] {'cand'}, dimensions={0} | all-to-all | bytes 65536 | tf_op jit(solution)/shard_map/all_to_all | solution.py:411
  55.7 0.0 copy-done.5
  55.7 0.1 broadcast_in_dim.11.rest_0_
  55.8 10.2 %rollout_1.1 = (f32[2,128]{1,0:T(2,128)S(1)}, f32[8,8,128]{2,1,0:T(8,128)S(1)}, f32[8,128]{1,0:T(8,128)S(1)}, f32[2,128]{1,0:T(2,128)S(1)}) custom-call(bf16[256,1024]{1,0:T(8,128)(2,1)S(1)} %get-tuple-element.48.w_h, bf16[256,768]{1,0:T(8,128)(2,1)S(1)} %get-tuple-element.49.w_x, bf16[128,256]{1,0:T(8,128)(2,1)S(1)} %get-tuple-element.50.w_1, ...), custom_call_target="tpu_custom_call" | custom-call | tf_op jit(solution)/shard_map/rollout_1/pallas_call | solution.py:229
  66.0 7.8 %all_to_all.21.rest_1_ = f32[8,8,128]{2,1,0:T(8,128)S(1)} all-to-all(f32[8,8,128]{2,1,0:T(8,128)S(1)} %get-tuple-element.62), channel_id=1, replica_groups=mesh['env'=32,'cand'=8] {'cand'}, dimensions={0} | all-to-all | bytes 65536 | tf_op jit(solution)/shard_map/all_to_all | solution.py:411
  73.8 10.2 %rollout_2.1 = (f32[2,128]{1,0:T(2,128)S(1)}, f32[8,8,128]{2,1,0:T(8,128)S(1)}, f32[8,128]{1,0:T(8,128)S(1)}, f32[2,128]{1,0:T(2,128)S(1)}) custom-call(bf16[256,1024]{1,0:T(8,128)(2,1)S(1)} %get-tuple-element.48.w_h, bf16[256,768]{1,0:T(8,128)(2,1)S(1)} %get-tuple-element.49.w_x, bf16[128,256]{1,0:T(8,128)(2,1)S(1)} %get-tuple-element.50.w_1, ...), custom_call_target="tpu_custom_call" | custom-call | tf_op jit(solution)/shard_map/rollout_2/pallas_call | solution.py:229
  84.1 7.8 %all_to_all.22.got_ref = f32[8,8,128]{2,1,0:T(8,128)S(1)} all-to-all(f32[8,8,128]{2,1,0:T(8,128)S(1)} %get-tuple-element.64), channel_id=1, replica_groups=mesh['env'=32,'cand'=8] {'cand'}, dimensions={0} | all-to-all | bytes 65536 | tf_op jit(solution)/shard_map/all_to_all | solution.py:411
  91.9 1.0 %last.1 = (f32[6,2,12]{2,1,0:T(2,128)}, f32[6,2,12]{2,1,0:T(2,128)}, f32[3,2,128]{2,1,0:T(2,128)}, f32[2,3]{1,0:T(2,128)}) custom-call(f32[8,128]{1,0:T(8,128)S(1)} %get-tuple-element.63.state_ref, f32[8,8,128]{2,1,0:T(8,128)S(1)} %all_to_all.22.got_ref, f32[2,128]{1,0:T(2,128)S(1)} %get-tuple-element.65.r0, f32[2,128]{1,0:T(2,128)S(1)} %get-tuple-element.66.r1, ...), custom_call_target="tpu_custom_call" | custom-call | tf_op jit(solution)/shard_map/last/pallas_call | solution.py:412
  (9 shorter events, 0.1 us)
Async XLA Ops:
  0.7 0.7 copy-start.1
  2.3 21.0 %all-to-all-start = ((bf16[32,8,256]{2,1,0:T(8,128)(2,1)}), bf16[32,8,256]{2,1,0:T(8,128)(2,1)S(1)}, u32[]{:S(2)}, u32[]{:S(2)}) async-start(bf16[32,8,256]{2,1,0:T(8,128)(2,1)} %broadcast_in_dim.9), calls=%async_computation | async-start | bytes 262144 | tf_op jit(solution)/shard_map/all_to_all | solution.py:370
  14.2 13.0 %copy-start.3 = (f32[2,200]{1,0:T(2,128)S(1)}, f32[2,200]{1,0:T(2,128)}, u32[]{:S(2)}) copy-start(f32[2,200]{1,0:T(2,128)} %param.8) | copy-start | bytes 4804
  14.3 12.9 %copy-start.2 = (s32[3,2,100]{2,1,0:T(2,128)S(1)}, s32[3,2,100]{2,1,0:T(2,128)}, u32[]{:S(2)}) copy-start(s32[3,2,100]{2,1,0:T(2,128)} %param.12) | copy-start | bytes 7204
  23.3 7.8 %collective-permute-start = (bf16[32,8,256]{2,1,0:T(8,128)(2,1)S(1)}, bf16[32,8,256]{2,1,0:T(8,128)(2,1)S(1)}, u32[]{:S(2)}, u32[]{:S(2)}) collective-permute-start(bf16[32,8,256]{2,1,0:T(8,128)(2,1)S(1)} %all-to-all-done), channel_id=1, source_target_pairs={{0,2},{1,3},{2,0},{3,1},{4,6},{5,7},{6,4},{7,5},{8,10},{9,11},{10,... | collective-permute-start | bytes 393224 | tf_op jit(solution)/shard_map/ppermute | solution.py:378
  24.6 6.6 %collective-permute-start.1 = (bf16[32,8,256]{2,1,0:T(8,128)(2,1)S(1)}, bf16[32,8,256]{2,1,0:T(8,128)(2,1)S(1)}, u32[]{:S(2)}, u32[]{:S(2)}) collective-permute-start(bf16[32,8,256]{2,1,0:T(8,128)(2,1)S(1)} %all-to-all-done), channel_id=1, source_target_pairs={{0,4},{1,5},{2,6},{3,7},{4,0},{5,1},{6,2},{7,3},{8,12},{9,13},{10,... | collective-permute-start | bytes 393224 | tf_op jit(solution)/shard_map/ppermute | solution.py:378
  27.2 5.5 %collective-permute-start.2 = (bf16[32,8,256]{2,1,0:T(8,128)(2,1)S(1)}, bf16[32,8,256]{2,1,0:T(8,128)(2,1)S(1)}, u32[]{:S(2)}, u32[]{:S(2)}) collective-permute-start(bf16[32,8,256]{2,1,0:T(8,128)(2,1)S(1)} %all-to-all-done), channel_id=1, source_target_pairs={{0,6},{1,7},{2,4},{3,5},{4,2},{5,3},{6,0},{7,1},{8,14},{9,15},{10,... | collective-permute-start | bytes 393224 | tf_op jit(solution)/shard_map/ppermute | solution.py:378
  29.5 0.9 copy-start
  30.4 0.7 copy-start.4
  32.8 5.1 %collective-permute-start.3 = (bf16[4,32,8,256]{3,2,1,0:T(8,128)(2,1)S(1)}, bf16[4,32,8,256]{3,2,1,0:T(8,128)(2,1)S(1)}, u32[]{:S(2)}, u32[]{:S(2)}) collective-permute-start(bf16[4,32,8,256]{3,2,1,0:T(8,128)(2,1)S(1)} %pad_maximum_fusion.own), channel_id=1, source_target_pairs={{0,1},{1,0},{2,3},{3,2},{4,5},{5,4},{6,7},{7,6},{8,9},{9,8},{10,11... | collective-permute-start | bytes 1572872 | tf_op jit(solution)/shard_map/ppermute | solution.py:397
  48.2 7.5 %copy-start.5 = (f32[8]{0:T(128)S(1)}, f32[8]{0:T(128)}, u32[]{:S(2)}) copy-start(f32[8]{0:T(128)} %constant.40.clone) | copy-start | bytes 100

commit v6 on v5

--- a/solution.py
+++ b/solution.py
@@ -134,8 +134,8 @@
         gates = dot(x, w_x[:, :512]) + dot(hd, w_h[:, :512])
         half = 0.5 * h
         rh = (half + jnp.tanh(gates[:, :256] * (0.5 * S400)) * half).astype(BF16)
+        proposal = jnp.tanh((dot(x, w_x[:, 512:]) + dot(rh, w_r[...])) * S400)
         update = 0.5 + 0.5 * jnp.tanh(gates[:, 256:] * (0.5 * S400))
-        proposal = jnp.tanh((dot(x, w_x[:, 512:]) + dot(rh, w_r[...])) * S400)
         h = proposal + update * (h - proposal)
         if t > 0:
             q = scaled_elu(dot(hd, w_h[:, 768:]) + dot(za[:, :48], w_6z[:48]), S230)

time: 93.3 us -> 93.3 us (level)
  no operation moved by 1% of the time
where the time goes in v6:
time: 93.3 us; the launch traced here: 92.9 us
  Pallas kernels  31.8 us (34%)
  blocking collectives  23.1 us (25%)
  starting transfers between devices  19.4 us (21%)
  waiting for transfers between devices  12.1 us (13%)
  local copies, waits for them, and re-layouts  5.5 us (6%)
    pallas_call x3, Pallas kernels, rollout(): pl.pallas_call(functools.partial(rollout_kernel, first, number), out_shap...  30.2 us
    all_to_all x3, blocking collectives, body(): got = lax.all_to_all(out[1], 'cand', 0, 0, tiled=True)  23.1 us
    all_to_all x1, starting transfers between devices, from_env(): lax.all_to_all(jnp.broadcast_to(block[None], (32, 8, 256)), 'env', 0, 0,...  11.9 us
    all_to_all x1, waiting for transfers between devices, from_env(): lax.all_to_all(jnp.broadcast_to(block[None], (32, 8, 256)), 'env', 0, 0,...  8.98 us
    ppermute x3, starting transfers between devices, body(): lax.ppermute(block, 'cand', [(i, i ^ 2 * k) for i in range(PEERS)])  3.92 us
    ppermute x1, starting transfers between devices, body(): other = lax.ppermute(own, 'cand', [(i, i ^ 1) for i in range(PEERS)])  3.57 us
    unnamed x12, local copies, waits for them, and re-layouts  2.13 us
    reshape x1, local copies, waits for them, and re-layouts, body(): state_noise.reshape(ITERS, HOR, STOCH, COLS)  2.05 us
  transfers between devices with their start and end apart: 5, of which 4 were waited for; matrix products, arithmetic and copies ran while one was open for 3% of the time, Pallas kernels for 0%

profile of v6, /device:TPU:1, one launch (start us, length us, event | category | flops | bytes accessed | tf_op | source)
XLA Modules:
  0.0 92.9 jit_solution(8776840496292366976)
XLA Ops:
  0.7 0.0 copy-start.1
  0.7 0.7 copy-done.1
  1.3 0.2 dynamic_update_slice.3
  1.5 0.1 reshape.27
  1.6 0.7 broadcast_in_dim.9
  2.3 11.9 %all-to-all-start = ((bf16[32,8,256]{2,1,0:T(8,128)(2,1)}), bf16[32,8,256]{2,1,0:T(8,128)(2,1)S(1)}, u32[]{:S(2)}, u32[]{:S(2)}) async-start(bf16[32,8,256]{2,1,0:T(8,128)(2,1)} %broadcast_in_dim.9), calls=%async_computation | async-start | bytes 262144 | tf_op jit(solution)/shard_map/all_to_all | solution.py:370
  14.2 0.1 pad.25.clone
  14.2 0.0 copy-start.3
  14.2 0.1 pad.26.clone
  14.3 0.0 copy-start.2
  14.3 9.0 %all-to-all-done = bf16[32,8,256]{2,1,0:T(8,128)(2,1)S(1)} async-done(((bf16[32,8,256]{2,1,0:T(8,128)(2,1)}), bf16[32,8,256]{2,1,0:T(8,128)(2,1)S(1)}, u32[]{:S(2)}, u32[]{:S(2)}) %all-to-all-start) | async-done | bytes 131104 | tf_op jit(solution)/shard_map/all_to_all | solution.py:370
  23.3 1.3 %collective-permute-start = (bf16[32,8,256]{2,1,0:T(8,128)(2,1)S(1)}, bf16[32,8,256]{2,1,0:T(8,128)(2,1)S(1)}, u32[]{:S(2)}, u32[]{:S(2)}) collective-permute-start(bf16[32,8,256]{2,1,0:T(8,128)(2,1)S(1)} %all-to-all-done), channel_id=1, source_target_pairs={{0,2},{1,3},{2,0},{3,1},{4,6},{5,7},{6,4},{7,5},{8,10},{9,11},{10,... | collective-permute-start | bytes 393224 | tf_op jit(solution)/shard_map/ppermute | solution.py:378
  24.6 2.6 %collective-permute-start.1 = (bf16[32,8,256]{2,1,0:T(8,128)(2,1)S(1)}, bf16[32,8,256]{2,1,0:T(8,128)(2,1)S(1)}, u32[]{:S(2)}, u32[]{:S(2)}) collective-permute-start(bf16[32,8,256]{2,1,0:T(8,128)(2,1)S(1)} %all-to-all-done), channel_id=1, source_target_pairs={{0,4},{1,5},{2,6},{3,7},{4,0},{5,1},{6,2},{7,3},{8,12},{9,13},{10,... | collective-permute-start | bytes 393224 | tf_op jit(solution)/shard_map/ppermute | solution.py:378
  27.2 0.0 collective-permute-start.2
  27.2 0.0 copy-done.3
  27.2 0.0 copy-done.2
  27.2 0.2 compare_reduce_fusion
  27.4 2.0 %reshape.30 = bf16[3,12,30,256]{3,2,1,0:T(8,128)(2,1)S(1)} reshape(bf16[3,12,30,2,128]{4,3,2,1,0:T(2,128)(2,1)} %param.11) | data formatting | bytes 1105920 | tf_op jit(solution)/shard_map/reshape | solution.py:383
  29.5 0.0 copy-start
  29.5 0.1 pad.18.s_noise
  29.6 0.8 copy-done
  30.4 0.0 copy-start.4
  30.4 0.1 reshape.28
  30.5 0.6 copy-done.4
  31.1 0.0 collective-permute-done
  31.1 0.1 collective-permute-done.1
  31.2 1.5 %collective-permute-done.2 = bf16[32,8,256]{2,1,0:T(8,128)(2,1)S(1)} collective-permute-done((bf16[32,8,256]{2,1,0:T(8,128)(2,1)S(1)}, bf16[32,8,256]{2,1,0:T(8,128)(2,1)S(1)}, u32[]{:S(2)}, u32[]{:S(2)}) %collective-permute-start.2) | collective-permute-done | bytes 131104 | tf_op jit(solution)/shard_map/ppermute | solution.py:378
  32.7 0.1 pad_maximum_fusion.own
  32.8 3.6 %collective-permute-start.3 = (bf16[4,32,8,256]{3,2,1,0:T(8,128)(2,1)S(1)}, bf16[4,32,8,256]{3,2,1,0:T(8,128)(2,1)S(1)}, u32[]{:S(2)}, u32[]{:S(2)}) collective-permute-start(bf16[4,32,8,256]{3,2,1,0:T(8,128)(2,1)S(1)} %pad_maximum_fusion.own), channel_id=1, source_target_pairs={{0,1},{1,0},{2,3},{3,2},{4,5},{5,4},{6,7},{7,6},{8,9},{9,8},{10,11... | collective-permute-start | bytes 1572872 | tf_op jit(solution)/shard_map/ppermute | solution.py:397
  36.4 1.5 %collective-permute-done.3.other = bf16[4,32,8,256]{3,2,1,0:T(8,128)(2,1)S(1)} collective-permute-done((bf16[4,32,8,256]{3,2,1,0:T(8,128)(2,1)S(1)}, bf16[4,32,8,256]{3,2,1,0:T(8,128)(2,1)S(1)}, u32[]{:S(2)}, u32[]{:S(2)}) %collective-permute-start.3) | collective-permute-done | bytes 524320 | tf_op jit(solution)/shard_map/ppermute | solution.py:397
  37.9 0.6 prepare.1
  38.5 9.7 %rollout_0.1 = (f32[2,128]{1,0:T(2,128)S(1)}, f32[8,8,128]{2,1,0:T(8,128)S(1)}) custom-call(bf16[256,1024]{1,0:T(8,128)(2,1)S(1)} %get-tuple-element.48.w_h, bf16[256,768]{1,0:T(8,128)(2,1)S(1)} %get-tuple-element.49.w_x, bf16[128,256]{1,0:T(8,128)(2,1)S(1)} %get-tuple-element.50.w_1, bf16[256,256]{1,0:T(8,128)(2,1)S(1)} %get-tuple-element.51.w_5, ...), custom_call_target="tpu_custom_call" | custom-call | tf_op jit(solution)/shard_map/rollout_0/pallas_call | solution.py:229
  48.2 0.0 copy-start.5
  48.2 7.5 %all_to_all.20.rest_1_ = f32[8,8,128]{2,1,0:T(8,128)S(1)} all-to-all(f32[8,8,128]{2,1,0:T(8,128)S(1)} %get-tuple-element.60), channel_id=1, replica_groups=mesh['env'=32,'cand'=8] {'cand'}, dimensions={0} | all-to-all | bytes 65536 | tf_op jit(solution)/shard_map/all_to_all | solution.py:411
  55.7 0.0 copy-done.5
  55.7 0.1 broadcast_in_dim.11.rest_0_
  55.8 10.2 %rollout_1.1 = (f32[2,128]{1,0:T(2,128)S(1)}, f32[8,8,128]{2,1,0:T(8,128)S(1)}, f32[8,128]{1,0:T(8,128)S(1)}, f32[2,128]{1,0:T(2,128)S(1)}) custom-call(bf16[256,1024]{1,0:T(8,128)(2,1)S(1)} %get-tuple-element.48.w_h, bf16[256,768]{1,0:T(8,128)(2,1)S(1)} %get-tuple-element.49.w_x, bf16[128,256]{1,0:T(8,128)(2,1)S(1)} %get-tuple-element.50.w_1, ...), custom_call_target="tpu_custom_call" | custom-call | tf_op jit(solution)/shard_map/rollout_1/pallas_call | solution.py:229
  66.0 7.8 %all_to_all.21.rest_1_ = f32[8,8,128]{2,1,0:T(8,128)S(1)} all-to-all(f32[8,8,128]{2,1,0:T(8,128)S(1)} %get-tuple-element.62), channel_id=1, replica_groups=mesh['env'=32,'cand'=8] {'cand'}, dimensions={0} | all-to-all | bytes 65536 | tf_op jit(solution)/shard_map/all_to_all | solution.py:411
  73.8 10.2 %rollout_2.1 = (f32[2,128]{1,0:T(2,128)S(1)}, f32[8,8,128]{2,1,0:T(8,128)S(1)}, f32[8,128]{1,0:T(8,128)S(1)}, f32[2,128]{1,0:T(2,128)S(1)}) custom-call(bf16[256,1024]{1,0:T(8,128)(2,1)S(1)} %get-tuple-element.48.w_h, bf16[256,768]{1,0:T(8,128)(2,1)S(1)} %get-tuple-element.49.w_x, bf16[128,256]{1,0:T(8,128)(2,1)S(1)} %get-tuple-element.50.w_1, ...), custom_call_target="tpu_custom_call" | custom-call | tf_op jit(solution)/shard_map/rollout_2/pallas_call | solution.py:229
  84.1 7.8 %all_to_all.22.got_ref = f32[8,8,128]{2,1,0:T(8,128)S(1)} all-to-all(f32[8,8,128]{2,1,0:T(8,128)S(1)} %get-tuple-element.64), channel_id=1, replica_groups=mesh['env'=32,'cand'=8] {'cand'}, dimensions={0} | all-to-all | bytes 65536 | tf_op jit(solution)/shard_map/all_to_all | solution.py:411
  91.9 1.0 %last.1 = (f32[6,2,12]{2,1,0:T(2,128)}, f32[6,2,12]{2,1,0:T(2,128)}, f32[3,2,128]{2,1,0:T(2,128)}, f32[2,3]{1,0:T(2,128)}) custom-call(f32[8,128]{1,0:T(8,128)S(1)} %get-tuple-element.63.state_ref, f32[8,8,128]{2,1,0:T(8,128)S(1)} %all_to_all.22.got_ref, f32[2,128]{1,0:T(2,128)S(1)} %get-tuple-element.65.r0, f32[2,128]{1,0:T(2,128)S(1)} %get-tuple-element.66.r1, ...), custom_call_target="tpu_custom_call" | custom-call | tf_op jit(solution)/shard_map/last/pallas_call | solution.py:412
  (9 shorter events, 0.1 us)
Async XLA Ops:
  0.7 0.7 copy-start.1
  2.3 21.0 %all-to-all-start = ((bf16[32,8,256]{2,1,0:T(8,128)(2,1)}), bf16[32,8,256]{2,1,0:T(8,128)(2,1)S(1)}, u32[]{:S(2)}, u32[]{:S(2)}) async-start(bf16[32,8,256]{2,1,0:T(8,128)(2,1)} %broadcast_in_dim.9), calls=%async_computation | async-start | bytes 262144 | tf_op jit(solution)/shard_map/all_to_all | solution.py:370
  14.2 13.0 %copy-start.3 = (f32[2,200]{1,0:T(2,128)S(1)}, f32[2,200]{1,0:T(2,128)}, u32[]{:S(2)}) copy-start(f32[2,200]{1,0:T(2,128)} %param.8) | copy-start | bytes 4804
  14.3 12.9 %copy-start.2 = (s32[3,2,100]{2,1,0:T(2,128)S(1)}, s32[3,2,100]{2,1,0:T(2,128)}, u32[]{:S(2)}) copy-start(s32[3,2,100]{2,1,0:T(2,128)} %param.12) | copy-start | bytes 7204
  23.3 7.8 %collective-permute-start = (bf16[32,8,256]{2,1,0:T(8,128)(2,1)S(1)}, bf16[32,8,256]{2,1,0:T(8,128)(2,1)S(1)}, u32[]{:S(2)}, u32[]{:S(2)}) collective-permute-start(bf16[32,8,256]{2,1,0:T(8,128)(2,1)S(1)} %all-to-all-done), channel_id=1, source_target_pairs={{0,2},{1,3},{2,0},{3,1},{4,6},{5,7},{6,4},{7,5},{8,10},{9,11},{10,... | collective-permute-start | bytes 393224 | tf_op jit(solution)/shard_map/ppermute | solution.py:378
  24.6 6.6 %collective-permute-start.1 = (bf16[32,8,256]{2,1,0:T(8,128)(2,1)S(1)}, bf16[32,8,256]{2,1,0:T(8,128)(2,1)S(1)}, u32[]{:S(2)}, u32[]{:S(2)}) collective-permute-start(bf16[32,8,256]{2,1,0:T(8,128)(2,1)S(1)} %all-to-all-done), channel_id=1, source_target_pairs={{0,4},{1,5},{2,6},{3,7},{4,0},{5,1},{6,2},{7,3},{8,12},{9,13},{10,... | collective-permute-start | bytes 393224 | tf_op jit(solution)/shard_map/ppermute | solution.py:378
  27.2 5.5 %collective-permute-start.2 = (bf16[32,8,256]{2,1,0:T(8,128)(2,1)S(1)}, bf16[32,8,256]{2,1,0:T(8,128)(2,1)S(1)}, u32[]{:S(2)}, u32[]{:S(2)}) collective-permute-start(bf16[32,8,256]{2,1,0:T(8,128)(2,1)S(1)} %all-to-all-done), channel_id=1, source_target_pairs={{0,6},{1,7},{2,4},{3,5},{4,2},{5,3},{6,0},{7,1},{8,14},{9,15},{10,... | collective-permute-start | bytes 393224 | tf_op jit(solution)/shard_map/ppermute | solution.py:378
  29.5 0.9 copy-start
  30.4 0.7 copy-start.4
  32.8 5.1 %collective-permute-start.3 = (bf16[4,32,8,256]{3,2,1,0:T(8,128)(2,1)S(1)}, bf16[4,32,8,256]{3,2,1,0:T(8,128)(2,1)S(1)}, u32[]{:S(2)}, u32[]{:S(2)}) collective-permute-start(bf16[4,32,8,256]{3,2,1,0:T(8,128)(2,1)S(1)} %pad_maximum_fusion.own), channel_id=1, source_target_pairs={{0,1},{1,0},{2,3},{3,2},{4,5},{5,4},{6,7},{7,6},{8,9},{9,8},{10,11... | collective-permute-start | bytes 1572872 | tf_op jit(solution)/shard_map/ppermute | solution.py:397
  48.2 7.5 %copy-start.5 = (f32[8]{0:T(128)S(1)}, f32[8]{0:T(128)}, u32[]{:S(2)}) copy-start(f32[8]{0:T(128)} %constant.40.clone) | copy-start | bytes 100
